TPU v7x, 256 devices: a whole 4x4x8 slice. The times are simulated.
256 devices in a mesh: prow: 8 (over z), pcol: 32 (over x, y, core).
Axes of the slice: x: 4, y: 4, z: 8, core: 2. Of those that a mesh axis runs over, the one named last changes fastest.
Arguments:
- matrix: bfloat16 [8, 2048, 2, 8192], P(None, 'prow', None, 'pcol'), may hold values from -6 to 6
- pivots: int32 [4, 256], replicated, may hold values from 0 to 16383, as said below
- lower_inverse: bfloat16 [4, 256, 256], replicated, as said below
- upper_inverse: bfloat16 [4, 256, 256], replicated, as said below
Outputs:
- factored: bfloat16 [8, 2048, 2, 8192], P(None, 'prow', None, 'pcol')
Inputs may be any that keep to these rules, and one draw needn't show every extreme that they name: For step s and each i, pivots[s, i] is either s * 256 + i or a row index of s * 256 + 256 or more; the pivots of one step that differ from s * 256 + i are distinct. lower_inverse[s] is unit lower triangular. upper_inverse[s] is upper triangular.
All inputs are finite; a program needn't handle non-finite values.
Results may differ from a plain program's by a relative error of at most 0.0071.
Values may be sent and summed in bfloat16 or wider, within the bound.
A program may use at most 64 MiB of HBM per device.

v0:
```python
import jax
import jax.numpy as jnp
from jax import lax
from jax.sharding import PartitionSpec as P


def spread(value, axis, source):
    kept = jnp.where(lax.axis_index(axis) == source, value, 0).astype(value.dtype)
    return lax.psum(kept, axis)


def local(matrix, pivots, lower_inverse, upper_inverse):
    row_blocks = matrix.shape[0]
    block_size = matrix.shape[1]
    col_blocks = matrix.shape[2]
    local_rows = row_blocks * block_size
    local_cols = col_blocks * block_size
    matrix_loc = matrix.reshape(local_rows, local_cols)
    row_count = lax.axis_size("prow")
    col_count = lax.axis_size("pcol")
    my_row = lax.axis_index("prow")
    my_col = lax.axis_index("pcol")
    row_iota = jnp.arange(local_rows, dtype=jnp.int32)
    col_iota = jnp.arange(local_cols, dtype=jnp.int32)
    global_row = (row_iota // block_size * row_count + my_row) * block_size + row_iota % block_size
    global_col = (col_iota // block_size * col_count + my_col) * block_size + col_iota % block_size
    for step_num in range(pivots.shape[0]):
        begin_at = step_num * block_size
        trail_at = begin_at + block_size
        diag_root = step_num % row_count
        diag_local = step_num // row_count * block_size
        panel_root = step_num % col_count
        panel_local = step_num // col_count * block_size
        targets = begin_at + jnp.arange(block_size, dtype=jnp.int32)
        chosen = pivots[step_num]
        chosen_block = chosen // block_size
        chosen_owner = chosen_block % row_count
        is_mine = chosen_owner == my_row
        chosen_local = chosen_block // row_count * block_size + chosen % block_size
        picked = jnp.take(matrix_loc, jnp.where(is_mine, chosen_local, 0), axis=0)
        picked = jnp.where(is_mine[:, None], picked, jnp.zeros_like(picked))
        diag_rows = matrix_loc[diag_local : diag_local + block_size]
        gathered = lax.all_gather(picked, "prow", axis=0, tiled=True)
        stacked = gathered.reshape(row_count, block_size, local_cols)
        owner_hit = jnp.arange(row_count, dtype=jnp.int32)[:, None] == chosen_owner[None, :]
        new_rows = jnp.sum(
            jnp.where(owner_hit[:, :, None], stacked, jnp.zeros_like(stacked)), axis=0
        )
        old_diag = spread(diag_rows, "prow", diag_root)
        moved_rows = is_mine & (chosen != targets)
        matrix_loc = matrix_loc.at[jnp.where(moved_rows, chosen_local, local_rows)].set(
            old_diag, mode="drop"
        )
        diag_after = matrix_loc[diag_local : diag_local + block_size]
        matrix_loc = matrix_loc.at[diag_local : diag_local + block_size].set(
            jnp.where(my_row == diag_root, new_rows, diag_after)
        )
        upper_full = jnp.dot(
            lower_inverse[step_num], new_rows, preferred_element_type=jnp.float32
        ).astype(jnp.bfloat16)
        col_live = global_col >= trail_at
        upper_use = jnp.where(col_live[None, :], upper_full, jnp.zeros_like(upper_full))
        panel_own = matrix_loc[:, panel_local : panel_local + block_size]
        received = spread(panel_own, "pcol", panel_root)
        left_full = jnp.dot(
            received, upper_inverse[step_num], preferred_element_type=jnp.float32
        ).astype(jnp.bfloat16)
        row_live = global_row >= trail_at
        left_use = jnp.where(row_live[:, None], left_full, jnp.zeros_like(left_full))
        matrix_loc = (
            matrix_loc.astype(jnp.float32)
            - jnp.dot(left_use, upper_use, preferred_element_type=jnp.float32)
        ).astype(jnp.bfloat16)
        panel_now = matrix_loc[:, panel_local : panel_local + block_size]
        panel_put = jnp.where(row_live[:, None] & (my_col == panel_root), left_full, panel_now)
        matrix_loc = matrix_loc.at[:, panel_local : panel_local + block_size].set(panel_put)
        diag_now = matrix_loc[diag_local : diag_local + block_size]
        diag_put = jnp.where(col_live[None, :] & (my_row == diag_root), upper_full, diag_now)
        matrix_loc = matrix_loc.at[diag_local : diag_local + block_size].set(diag_put)
    return matrix_loc.reshape(matrix.shape)


def solution(mesh):
    placed = (P(None, "prow", None, "pcol"), P(), P(), P())
    return jax.shard_map(
        local, mesh=mesh, in_specs=placed, out_specs=P(None, "prow", None, "pcol"), check_vma=False
    )
```

profile of v0, /device:TPU:1, one launch (start us, length us, event | category | flops | bytes accessed | tf_op | source)
XLA Modules:
  0.0 982.3 jit_solution(12199594610326055330)
XLA Ops:
  6.5 1.2 broadcast_select_fusion
  8.5 0.9 and_select_fusion
  9.4 2.0 copy.17
  11.5 1.2 gather_fusion
  14.4 66.9 %all-reduce.9.cloned.1.call-done = bf16[256,512]{1,0:T(8,128)(2,1)} async-done(((bf16[256,512]{1,0:T(8,128)(2,1)}), bf16[256,512]{1,0:T(8,128)(2,1)}) %all-reduce.9.cloned.1.call-update) | async-done | bytes 262160 | tf_op jit(solution)/shard_map/psum | solution.py:9
  81.3 3.1 scatter_fusion
  84.4 38.9 %all-gather.5.cloned.1.call-done = bf16[2048,512]{1,0:T(8,128)(2,1)} async-done(((bf16[256,512]{1,0:T(8,128)(2,1)}), bf16[2048,512]{1,0:T(8,128)(2,1)}) %all-gather.5.cloned.1.call-update) | async-done | bytes 2097168 | tf_op jit(solution)/shard_map/all_gather | solution.py:43
  123.4 1.9 select_reduce_fusion.3
  125.3 1.0 slice_select_fusion.3
  126.7 118.0 %all-reduce.11.cloned.1.call-done = bf16[2048,256]{1,0:T(8,128)(2,1)} async-done(((bf16[2048,256]{1,0:T(8,128)(2,1)}), bf16[2048,256]{1,0:T(8,128)(2,1)}) %all-reduce.11.cloned.1.call-update) | async-done | bytes 1048592 | tf_op jit(solution)/shard_map/psum | solution.py:9
  244.7 1.6 convolution_convert_fusion.3
  246.4 2.0 subtract_convert_fusion.3
  248.4 3.4 fusion.4
  251.8 1.8 broadcast_select_fusion.3
  253.7 3.1 gather_fusion.1
  257.8 63.7 %all-reduce.13.cloned.1.call-done = bf16[256,512]{1,0:T(8,128)(2,1)} async-done(((bf16[256,512]{1,0:T(8,128)(2,1)}), bf16[256,512]{1,0:T(8,128)(2,1)}) %all-reduce.13.cloned.1.call-update) | async-done | bytes 262160 | tf_op jit(solution)/shard_map/psum | solution.py:9
  321.5 5.2 scatter_fusion.1
  326.7 36.7 %all-gather.7.cloned.1.call-done = bf16[2048,512]{1,0:T(8,128)(2,1)} async-done(((bf16[256,512]{1,0:T(8,128)(2,1)}), bf16[2048,512]{1,0:T(8,128)(2,1)}) %all-gather.7.cloned.1.call-update) | async-done | bytes 2097168 | tf_op jit(solution)/shard_map/all_gather | solution.py:43
  363.4 1.9 select_reduce_fusion.2
  365.2 1.7 fusion.23
  367.0 2.3 slice_select_fusion.2
  369.6 118.0 %all-reduce.15.cloned.1.call-done = bf16[2048,256]{1,0:T(8,128)(2,1)} async-done(((bf16[2048,256]{1,0:T(8,128)(2,1)}), bf16[2048,256]{1,0:T(8,128)(2,1)}) %all-reduce.15.cloned.1.call-update) | async-done | bytes 1048592 | tf_op jit(solution)/shard_map/psum | solution.py:9
  487.6 1.6 convolution_convert_fusion.2
  489.3 2.3 subtract_convert_fusion.2
  491.5 1.5 fusion.5
  494.1 1.2 gather_fusion.2
  496.2 65.4 %all-reduce.17.cloned.1.call-done = bf16[256,512]{1,0:T(8,128)(2,1)} async-done(((bf16[256,512]{1,0:T(8,128)(2,1)}), bf16[256,512]{1,0:T(8,128)(2,1)}) %all-reduce.17.cloned.1.call-update) | async-done | bytes 262160 | tf_op jit(solution)/shard_map/psum | solution.py:9
  561.6 3.1 scatter_fusion.2
  564.7 38.9 %all-gather.9.cloned.1.call-done = bf16[2048,512]{1,0:T(8,128)(2,1)} async-done(((bf16[256,512]{1,0:T(8,128)(2,1)}), bf16[2048,512]{1,0:T(8,128)(2,1)}) %all-gather.9.cloned.1.call-update) | async-done | bytes 2097168 | tf_op jit(solution)/shard_map/all_gather | solution.py:43
  603.6 1.9 select_reduce_fusion.1
  605.6 1.0 slice_select_fusion.1
  607.0 118.0 %all-reduce.19.cloned.1.call-done = bf16[2048,256]{1,0:T(8,128)(2,1)} async-done(((bf16[2048,256]{1,0:T(8,128)(2,1)}), bf16[2048,256]{1,0:T(8,128)(2,1)}) %all-reduce.19.cloned.1.call-update) | async-done | bytes 1048592 | tf_op jit(solution)/shard_map/psum | solution.py:9
  725.0 1.7 convolution_convert_fusion.1
  726.6 2.0 subtract_convert_fusion.1
  728.6 3.4 fusion.6
  732.0 1.8 broadcast_select_fusion.1
  734.0 3.1 gather_fusion.3
  738.0 63.7 %all-reduce.21.cloned.1.call-done = bf16[256,512]{1,0:T(8,128)(2,1)} async-done(((bf16[256,512]{1,0:T(8,128)(2,1)}), bf16[256,512]{1,0:T(8,128)(2,1)}) %all-reduce.21.cloned.1.call-update) | async-done | bytes 262160 | tf_op jit(solution)/shard_map/psum | solution.py:9
  801.7 5.2 scatter_fusion.3
  806.9 36.8 %all-gather.11.cloned.1.call-done = bf16[2048,512]{1,0:T(8,128)(2,1)} async-done(((bf16[256,512]{1,0:T(8,128)(2,1)}), bf16[2048,512]{1,0:T(8,128)(2,1)}) %all-gather.11.cloned.1.call-update) | async-done | bytes 2097168 | tf_op jit(solution)/shard_map/all_gather | solution.py:43
  843.8 1.9 select_reduce_fusion
  845.6 1.7 fusion.21
  847.4 2.3 slice_select_fusion
  850.0 118.0 %all-reduce.23.cloned.1.call-done = bf16[2048,256]{1,0:T(8,128)(2,1)} async-done(((bf16[2048,256]{1,0:T(8,128)(2,1)}), bf16[2048,256]{1,0:T(8,128)(2,1)}) %all-reduce.23.cloned.1.call-update) | async-done | bytes 1048592 | tf_op jit(solution)/shard_map/psum | solution.py:9
  968.0 1.6 convolution_convert_fusion
  969.7 2.3 subtract_convert_fusion
  971.9 1.5 fusion.7
  973.5 2.0 reshape.1320
  (69 shorter events, 8.0 us)
Async XLA Ops:
  6.5 74.8 %all-reduce.9.cloned.1.call-start = ((), (), s32[]{:S(2)}) async-start(), calls=%async_computation | async-start | bytes 524288 | tf_op jit(solution)/shard_map/psum | solution.py:9
  8.5 114.9 %all-gather.5.cloned.1.call-start = ((), (), s32[]{:S(2)}) async-start(), calls=%async_computation.1 | async-start | bytes 2359296 | tf_op jit(solution)/shard_map/all_gather | solution.py:43
  11.5 2.8 copy-start.1
  13.5 231.2 %all-reduce.11.cloned.1.call-start = ((), (), s32[]{:S(2)}) async-start(), calls=%async_computation.2 | async-start | bytes 2097152 | tf_op jit(solution)/shard_map/psum | solution.py:9
  125.2 1.3 copy-start
  126.4 195.1 %all-reduce.13.cloned.1.call-start = ((), (), s32[]{:S(2)}) async-start(), calls=%async_computation.3 | async-start | bytes 524288 | tf_op jit(solution)/shard_map/psum | solution.py:9
  253.6 109.7 %all-gather.7.cloned.1.call-start = ((), (), s32[]{:S(2)}) async-start(), calls=%async_computation.4 | async-start | bytes 2359296 | tf_op jit(solution)/shard_map/all_gather | solution.py:43
  257.6 230.0 %all-reduce.15.cloned.1.call-start = ((), (), s32[]{:S(2)}) async-start(), calls=%async_computation.5 | async-start | bytes 2097152 | tf_op jit(solution)/shard_map/psum | solution.py:9
  369.3 192.3 %all-reduce.17.cloned.1.call-start = ((), (), s32[]{:S(2)}) async-start(), calls=%async_computation.6 | async-start | bytes 524288 | tf_op jit(solution)/shard_map/psum | solution.py:9
  493.8 109.8 %all-gather.9.cloned.1.call-start = ((), (), s32[]{:S(2)}) async-start(), calls=%async_computation.7 | async-start | bytes 2359296 | tf_op jit(solution)/shard_map/all_gather | solution.py:43
  496.1 228.9 %all-reduce.19.cloned.1.call-start = ((), (), s32[]{:S(2)}) async-start(), calls=%async_computation.8 | async-start | bytes 2097152 | tf_op jit(solution)/shard_map/psum | solution.py:9
  606.7 195.1 %all-reduce.21.cloned.1.call-start = ((), (), s32[]{:S(2)}) async-start(), calls=%async_computation.9 | async-start | bytes 524288 | tf_op jit(solution)/shard_map/psum | solution.py:9
  733.9 109.9 %all-gather.11.cloned.1.call-start = ((), (), s32[]{:S(2)}) async-start(), calls=%async_computation.10 | async-start | bytes 2359296 | tf_op jit(solution)/shard_map/all_gather | solution.py:43
  737.9 230.1 %all-reduce.23.cloned.1.call-start = ((), (), s32[]{:S(2)}) async-start(), calls=%async_computation.11 | async-start | bytes 2097152 | tf_op jit(solution)/shard_map/psum | solution.py:9
Sparse Core Ops, SparseCore 0:
  9.6 71.6 all-reduce.8
  83.1 40.1 all-gather.4
  126.6 118.0 all-reduce.10
  253.8 67.6 all-reduce.12
  323.1 40.1 all-gather.6
  369.4 118.1 all-reduce.14
  494.0 67.5 all-reduce.16
  563.4 40.1 all-gather.8
  606.9 118.0 all-reduce.18
  734.0 67.6 all-reduce.20
  803.5 40.1 all-gather.10
  849.8 118.1 all-reduce.22
where the time goes:
time: 983 us; the launch traced here: 982 us
  waiting for transfers between devices  883 us (90%)
  other arithmetic  38.6 us (4%)
  local copies, waits for them, and re-layouts  29.8 us (3%)
  matrix products  16 us (2%)
  between operations  13.9 us (1%)
    psum x8, waiting for transfers between devices, spread(): return lax.psum(kept, axis)  732 us
    all_gather x4, waiting for transfers between devices, local(): gathered = lax.all_gather(picked, 'prow', axis=0, tiled=True)  151 us
  transfers between devices with their start and end apart: 12, of which 12 were waited for; matrix products, arithmetic and copies ran while one was open for 3% of the time, Pallas kernels for 0%

commit v1 on v0

v1 whole, which is shorter than its diff:
```python
import jax
import jax.numpy as jnp
from jax import lax
from jax.experimental import pallas as pl
from jax.experimental.pallas import tpu as pltpu
from jax.sharding import PartitionSpec as P

BF = jnp.bfloat16
F32 = jnp.float32
NB = 256
NZ = 8
TOP = 1024
COLS = 512


def dot(a, b):
    return jnp.dot(a, b, preferred_element_type=F32)


def kernel(a_ref, piv_ref, linv_ref, uinv_ref, out_ref,
           srcb, destr, contrib, rs_long, rs_short, top_own, old_own, pan, top_pan,
           left, tx, ux,
           sem_rs, rem_rs, sem_tz, rem_tz, sem_dz, rem_dz,
           sem_sc, rem_sc, sem_mir, rem_mir, loc_sem, sem_ds, rem_ds,
           sem_ts, rem_ts, sem_tsl, rem_tsl,
           sem_ring, rem_ring, sem_par, rem_par):
    r = lax.axis_index("prow")
    q = lax.axis_index("pcol")
    x = q // 8
    y = (q // 2) % 4
    core = q % 2
    g = core * 4 + x

    def panel_of(yy):
        return (yy % 3 + 1) * ((yy + 3) // 4)

    p = panel_of(y)
    home_y = ((q + 1) % 3 + 1) * ((q + 3) // 4)

    def dev(rr, qq):
        return (rr, qq)

    def at_q(xx, yy, cc):
        return xx * 8 + yy * 2 + cc

    def plane(off):
        return (r + off + NZ) % NZ

    def rcopy(src, dst, ssem, rsem, where):
        return pltpu.make_async_remote_copy(
            src_ref=src, dst_ref=dst, send_sem=ssem, recv_sem=rsem,
            device_id=where, device_id_type=pl.DeviceIdType.MESH)

    def got(dst, ssem, rsem, where):
        rcopy(dst, dst, ssem, rsem, where).wait_recv()

    def sent(src, ssem, rsem, where):
        rcopy(src, src, ssem, rsem, where).wait_send()

    x_up, x_dn = at_q((x + 1) % 4, y, core), at_q((x + 3) % 4, y, core)
    y_up, y_dn = at_q(x, (y + 1) % 4, core), at_q(x, (y + 3) % 4, core)
    mate = at_q(x, y, 1 - core)

    barrier = pltpu.get_barrier_semaphore()

    def greet(where):
        pl.semaphore_signal(barrier, inc=1, device_id=where, device_id_type=pl.DeviceIdType.MESH)

    for off in range(1, NZ):
        greet(dev(plane(off), q))
    for other in (x_up, x_dn, y_up, y_dn, mate):
        greet(dev(r, other))

    keeps = (q == 0) | (q == 2)
    gives = (q == 1) | (q == 3)

    @pl.when(jnp.logical_not(keeps))
    def _():
        greet(dev(r, p))

    @pl.when(gives)
    def _():
        greet(dev(r, at_q(0, home_y, 0)))

    @pl.when(q < 4)
    def _():
        for t in range(1, 8):
            greet(dev(r, at_q(t % 4, home_y, t // 4)))

    def colb(row):
        return jnp.transpose(jnp.broadcast_to(row, (128, 128)))

    pts = []
    for s in range(4):
        row = piv_ref[s:s + 1, :].astype(F32)
        pts.append(jnp.concatenate([colb(row[:, :128]), colb(row[:, 128:])], axis=0))
    sub = lax.broadcasted_iota(jnp.int32, (NB, 128), 0).astype(F32)
    lane = lax.broadcasted_iota(jnp.int32, (1, 128), 1).astype(F32)

    def swap(cur, s):
        target = sub + float(s * NB)
        delta = pts[s] - target
        move = jnp.where(target == cur, delta, 0.0) - jnp.where(pts[s] == cur, delta, 0.0)
        return cur + jnp.sum(move, axis=0, keepdims=True)

    def perm_tile(t, carry):
        start = lane + (t * 128).astype(F32)
        cur = start
        for s in (3, 2, 1, 0):
            cur = swap(cur, s)
        srcb[pl.ds(pl.multiple_of(t * 128, 128), 128), :] = colb(cur)
        cur = start
        for s in (0, 1, 2, 3):
            cur = swap(cur, s)
        destr[t] = cur
        return carry

    lax.fori_loop(0, 8, perm_tile, 0)

    @pl.when(keeps)
    def _():
        pl.semaphore_wait(barrier, 19)

    @pl.when(gives)
    def _():
        pl.semaphore_wait(barrier, 21)

    @pl.when(q >= 4)
    def _():
        pl.semaphore_wait(barrier, 13)

    def scatter_raw(t):
        tx_, tc = t % 4, t // 4
        return rcopy(a_ref.at[:, pl.ds(32 * t, 32), pl.ds(0, NB)],
                     pan.at[pl.ds(0, 8), pl.ds(32 * t, 32), pl.ds(pl.multiple_of(NB * q, NB), NB)],
                     sem_sc.at[t], rem_sc.at[0], dev(r, at_q(tx_, home_y, tc)))

    def raw_self():
        return pltpu.make_async_copy(a_ref.at[:, pl.ds(0, 32), pl.ds(0, NB)],
                                     pan.at[pl.ds(0, 8), pl.ds(0, 32), pl.ds(pl.multiple_of(NB * q, NB), NB)],
                                     loc_sem.at[0])

    @pl.when(keeps)
    def _():
        raw_self().start()

    @pl.when(gives)
    def _():
        scatter_raw(0).start()

    @pl.when(q < 4)
    def _():
        for t in range(1, 8):
            scatter_raw(t).start()

    def mirror():
        return rcopy(a_ref.at[0, pl.ds(128, 128), :],
                     old_own.at[r % 4, pl.ds(128, 128), :],
                     sem_mir.at[0], rem_mir.at[0], dev(7 - r, q))

    def old_self():
        return pltpu.make_async_copy(a_ref.at[0, pl.ds(0, 128), :],
                                     old_own.at[r % 4, pl.ds(0, 128), :], loc_sem.at[1])

    @pl.when(r < 4)
    def _():
        mirror().start()
        old_self().start()

    def contribute(i, carry):
        off = 4 + (i % 2) * ((i + 1) // 2) - (1 - i % 2) * (i // 2)
        chunk = (r + off) % NZ
        want = srcb[pl.ds(pl.multiple_of(chunk * 128, 128), 128), :]
        tiles = []
        for t in range(16):
            gid = lane + ((t // 2 * NZ + r) * NB + (t % 2) * 128).astype(F32)
            tiles.append(jnp.where(want == gid, 1.0, 0.0).astype(BF))
        pick = jnp.concatenate(tiles, axis=1)
        contrib[chunk] = dot(pick, a_ref[...].reshape(2048, COLS)).astype(BF)
        return carry

    def half(h):
        return pl.ds(NB * h, NB)

    def delta(h):
        return 1 if h == 0 else -1

    def rs_send(h, way, k):
        d = delta(h) if way == 0 else -delta(h)
        buf = rs_long if way == 0 else rs_short
        first = 4 if way == 0 else 3
        src = contrib.at[plane(first * d), :, half(h)] if k == 0 else buf.at[h, k - 1]
        idx = h * 7 + way * 4 + k
        return rcopy(src, buf.at[h, k], sem_rs.at[idx], rem_rs.at[idx], dev(plane(d), q))

    def rs_step(h, way, k):
        d = delta(h) if way == 0 else -delta(h)
        buf = rs_long if way == 0 else rs_short
        first = 4 if way == 0 else 3
        rs_send(h, way, k - 1).wait_recv()
        buf[h, k - 1] = buf[h, k - 1] + contrib[plane((first - k) * d), :, NB * h:NB * (h + 1)]
        rs_send(h, way, k).start()

    def rs_end(h):
        rs_send(h, 0, 3).wait_recv()
        rs_send(h, 1, 2).wait_recv()
        top_own[r, :, NB * h:NB * (h + 1)] = (
            contrib[r, :, NB * h:NB * (h + 1)] + rs_long[h, 3] + rs_short[h, 2])

    def top_view(j, h):
        return top_own.at[j, :, half(h)]

    def old_view(j, h):
        hi = j // 4
        a = j + hi * (7 - 2 * j)
        return old_own.at[a, pl.ds(pl.multiple_of(128 * hi, 128), 128), half(h)]

    def zag(view, ssem, rsem, h, way, k):
        d = delta(h) if way == 0 else -delta(h)
        idx = h * 7 + way * 4 + k
        v = view(plane(-k * d), h)
        return rcopy(v, v, ssem.at[idx], rsem.at[idx], dev(plane(d), q))

    def zag_got(view, ssem, rsem, h, way, k):
        d = delta(h) if way == 0 else -delta(h)
        idx = h * 7 + way * 4 + k
        got(view(plane(-(k + 1) * d), h), ssem.at[idx], rsem.at[idx], dev(plane(d), q))

    def zag_step(view, ssem, rsem, h, k):
        for way in range(2):
            if k < 4 - way:
                if k > 0:
                    zag_got(view, ssem, rsem, h, way, k - 1)
                zag(view, ssem, rsem, h, way, k).start()

    def zag_end(view, ssem, rsem, h):
        zag_got(view, ssem, rsem, h, 0, 3)
        zag_got(view, ssem, rsem, h, 1, 2)

    top_z = (top_view, sem_tz, rem_tz)
    old_z = (old_view, sem_dz, rem_dz)

    class Ring:
        def __init__(self, buf, n0, rows, base):
            self.buf, self.n0, self.rows, self.base = buf, n0, rows, base

        def reg(self, part, stage, j, piece=None):
            n0, rows = self.n0, self.rows
            lo, n = (0, n0 // 2) if part == 0 else (n0 // 2, n0 // 2)
            if piece is not None:
                n = n // 2
                lo = lo + n * piece
            k = pl.ds(lo, n)
            along_y = (part == 0) == (stage == 0)
            if stage == 0:
                col = panel_of(j) if along_y else p
                gg = g if along_y else core * 4 + j
                return self.buf.at[k, pl.ds(pl.multiple_of(rows * gg, rows), rows),
                                   pl.ds(pl.multiple_of(NB * col, NB), NB)]
            if part == 0:
                gg = core * 4 + j
                return self.buf.at[k, pl.ds(pl.multiple_of(rows * gg, rows), rows), :]
            return self.buf.at[k, pl.ds(pl.multiple_of(4 * rows * core, 4 * rows), 4 * rows),
                               pl.ds(pl.multiple_of(NB * panel_of(j), NB), NB)]

        def copy(self, part, stage, which):
            along_y = (part == 0) == (stage == 0)
            m = y if along_y else x
            up, dn = (y_up, y_dn) if along_y else (x_up, x_dn)
            idx = self.base + (part * 2 + stage) * 4 + which
            if which < 2:
                v = self.reg(part, stage, m)
            elif which == 2:
                v = self.reg(part, stage, (m + 3) % 4, 0)
            else:
                v = self.reg(part, stage, (m + 1) % 4, 1)
            return rcopy(v, v, sem_ring.at[idx], rem_ring.at[idx], dev(r, up if which % 2 == 0 else dn))

        def wait(self, part, stage, which):
            along_y = (part == 0) == (stage == 0)
            m = y if along_y else x
            idx = self.base + (part * 2 + stage) * 4 + which
            if which == 0:
                v = self.reg(part, stage, (m + 3) % 4)
            elif which == 1:
                v = self.reg(part, stage, (m + 1) % 4)
            else:
                v = self.reg(part, stage, (m + 2) % 4, which - 2)
            got(v, sem_ring.at[idx], rem_ring.at[idx], dev(r, mate))

        def par_view(self, part, piece):
            along_y = part == 1
            m = y if along_y else x
            return m, (0, 3, 1, 2)[piece]

        def par(self, part, piece):
            m, o = self.par_view(part, piece)
            v = self.reg(part, 1, (m + o) % 4)
            idx = self.base // 2 + part * 4 + piece
            return rcopy(v, v, sem_par.at[idx], rem_par.at[idx], dev(r, mate))

        def par_wait(self, part, piece):
            m, o = self.par_view(part, piece)
            v = self.reg_other(part, (m + o) % 4)
            idx = self.base // 2 + part * 4 + piece
            got(v, sem_par.at[idx], rem_par.at[idx], dev(r, mate))

        def reg_other(self, part, j):
            n0, rows = self.n0, self.rows
            oc = 1 - core
            if part == 0:
                gg = oc * 4 + j
                return self.buf.at[pl.ds(0, n0 // 2), pl.ds(pl.multiple_of(rows * gg, rows), rows), :]
            return self.buf.at[pl.ds(n0 // 2, n0 // 2),
                               pl.ds(pl.multiple_of(4 * rows * oc, 4 * rows), 4 * rows),
                               pl.ds(pl.multiple_of(NB * panel_of(j), NB), NB)]

        def start(self, stage):
            for part in range(2):
                self.copy(part, stage, 0).start()
                self.copy(part, stage, 1).start()

        def forward(self, stage):
            for part in range(2):
                self.wait(part, stage, 0)
                self.copy(part, stage, 2).start()
                self.wait(part, stage, 1)
                self.copy(part, stage, 3).start()
                if stage == 1:
                    self.par(part, 1).start()
                    self.par(part, 2).start()

        def finish(self, stage):
            for part in range(2):
                self.wait(part, stage, 2)
                self.wait(part, stage, 3)
                self.par(part, 0 if stage == 0 else 3).start()

        def close(self):
            for part in range(2):
                for piece in range(4):
                    self.par_wait(part, piece)

        def drain(self):
            for part in range(2):
                for stage in range(2):
                    for which in range(4):
                        self.copy(part, stage, which).wait_send()
                for piece in range(4):
                    self.par(part, piece).wait_send()

    ring_raw = Ring(pan, 12, 32, 0)
    ring_top = Ring(top_pan, 8, 16, 16)

    mine32 = pl.ds(pl.multiple_of(32 * g, 32), 32)
    mine16 = pl.ds(pl.multiple_of(16 * g, 16), 16)
    minec = pl.ds(pl.multiple_of(NB * p, NB), NB)

    def old_slice(off):
        return rcopy(pan.at[0, mine32, minec], pan.at[8 + r % 4, mine32, minec],
                     sem_ds.at[off - 1], rem_ds.at[r % 4], dev(plane(off), q))

    def old_slice_self():
        return pltpu.make_async_copy(pan.at[0, mine32, minec], pan.at[8 + r % 4, mine32, minec],
                                     loc_sem.at[2])

    def top_piece(t):
        return rcopy(top_own.at[r, pl.ds(16 * t, 16), pl.ds(0, NB)],
                     top_pan.at[r, pl.ds(16 * t, 16), pl.ds(pl.multiple_of(NB * q, NB), NB)],
                     sem_ts.at[t], rem_ts.at[0], dev(r, at_q(t % 4, home_y, t // 4)))

    def top_piece_self():
        return pltpu.make_async_copy(top_own.at[r, pl.ds(0, 16), pl.ds(0, NB)],
                                     top_pan.at[r, pl.ds(0, 16), pl.ds(pl.multiple_of(NB * q, NB), NB)],
                                     loc_sem.at[3])

    def top_slice(off):
        v = top_pan.at[r, mine16, minec]
        return rcopy(v, v, sem_tsl.at[off - 1], rem_tsl.at[r], dev(plane(off), q))

    lax.fori_loop(0, 3, contribute, 0)
    for h in range(2):
        rs_send(h, 0, 0).start()
        rs_send(h, 1, 0).start()
    lax.fori_loop(3, 8, contribute, 0)

    for h in range(2):
        rs_step(h, 0, 1)
        rs_step(h, 1, 1)

    @pl.when(keeps)
    def _():
        raw_self().wait()

    @pl.when(jnp.logical_not(keeps))
    def _():
        got(pan.at[pl.ds(0, 8), mine32, minec], sem_sc.at[0], rem_sc.at[0], dev(r, mate))

    @pl.when(r < 4)
    def _():
        old_slice_self().start()
        for off in range(1, NZ):
            old_slice(off).start()
        old_self().wait()

    @pl.when(r >= 4)
    def _():
        got(old_own.at[(7 - r) % 4, pl.ds(128, 128), :], sem_mir.at[0], rem_mir.at[0], dev(7 - r, q))

    for h in range(2):
        rs_step(h, 0, 2)
        rs_step(h, 1, 2)

    for h in range(2):
        zag_step(*old_z, h, 0)

    for a in range(4):
        @pl.when(r != a)
        def _():
            got(pan.at[8 + a, mine32, minec], sem_ds.at[0], rem_ds.at[a], dev(r, mate))

    @pl.when(r < 4)
    def _():
        old_slice_self().wait()

    ring_raw.start(0)

    for h in range(2):
        rs_step(h, 0, 3)

    rs_end(0)

    @pl.when(keeps)
    def _():
        top_piece_self().start()

    @pl.when(gives)
    def _():
        top_piece(0).start()

    @pl.when(q < 4)
    def _():
        for t in range(1, 8):
            top_piece(t).start()

    zag_step(*top_z, 0, 0)
    rs_end(1)
    zag_step(*top_z, 1, 0)

    for h in range(2):
        zag_step(*old_z, h, 1)

    ring_raw.forward(0)

    @pl.when(keeps)
    def _():
        top_piece_self().wait()

    @pl.when(jnp.logical_not(keeps))
    def _():
        got(top_pan.at[r, mine16, minec], sem_ts.at[0], rem_ts.at[0], dev(r, mate))

    for off in range(1, NZ):
        top_slice(off).start()

    for h in range(2):
        zag_step(*top_z, h, 1)
    for h in range(2):
        zag_step(*old_z, h, 2)

    for off in range(1, NZ):
        src = plane(off)
        got(top_pan.at[src, mine16, minec], sem_tsl.at[0], rem_tsl.at[src], dev(r, mate))

    ring_top.start(0)
    ring_raw.finish(0)
    ring_raw.start(1)

    for h in range(2):
        zag_step(*top_z, h, 2)
    for h in range(2):
        zag_step(*old_z, h, 3)

    ring_top.forward(0)
    ring_top.finish(0)
    ring_top.start(1)

    for h in range(2):
        zag_step(*top_z, h, 3)

    ring_raw.forward(1)
    ring_top.forward(1)
    for h in range(2):
        zag_end(*old_z, h)
        zag_end(*top_z, h)
    ring_raw.finish(1)
    ring_raw.close()

    row_id = lax.broadcasted_iota(jnp.int32, (NB, 1), 0).astype(F32)

    def displaced(k, carry):
        mine = row_id + ((k * NZ + r) * NB).astype(F32)
        tiles, seen = [], None
        for t in range(8):
            hit = jnp.where(destr[t] == mine, 1.0, 0.0)
            seen = hit if seen is None else seen + hit
            tiles.append(hit.astype(BF))
        pick = jnp.concatenate(tiles, axis=1)
        moved = jnp.sum(seen, axis=1, keepdims=True) > 0.5
        rows = dot(pick, pan[8:12].reshape(TOP, TOP))
        left[k] = jnp.where(moved, rows, pan[k].astype(F32)).astype(BF)
        rows = dot(pick, old_own[...].reshape(TOP, COLS))
        out_ref[k] = jnp.where(moved, rows, a_ref[k].astype(F32)).astype(BF)
        return carry

    lax.fori_loop(0, 8, displaced, 0)

    ring_top.finish(1)
    ring_top.close()

    tx[...] = top_pan[...].reshape(TOP, TOP)
    ux[...] = top_own[...].reshape(TOP, COLS)
    for s in range(4):
        b, e = s * NB, (s + 1) * NB
        u_own = dot(linv_ref[s], ux[b:e, :]).astype(BF)
        ux[b:e, :] = u_own
        if s < 3:
            l_top = dot(tx[e:, b:e], uinv_ref[s]).astype(BF)
            tx[e:, b:e] = l_top
            u_pan = dot(linv_ref[s], tx[b:e, e:]).astype(BF)
            tx[b:e, e:] = u_pan
            tx[e:, e:] = (tx[e:, e:].astype(F32) - dot(l_top, u_pan)).astype(BF)
            ux[e:, :] = (ux[e:, :].astype(F32) - dot(l_top, u_own)).astype(BF)

    mycol = pl.ds(pl.multiple_of(NB * jnp.minimum(q, 3), NB), NB)

    def below(k, carry):
        for s in range(4):
            b, e = s * NB, (s + 1) * NB
            l_row = dot(left[k, :, b:e], uinv_ref[s]).astype(BF)
            left[k, :, b:e] = l_row
            if s < 3:
                left[k, :, e:] = (left[k, :, e:].astype(F32) - dot(l_row, tx[b:e, e:])).astype(BF)
        out_ref[k] = (out_ref[k].astype(F32) - dot(left[k], ux[...])).astype(BF)

        @pl.when(q < 4)
        def _():
            out_ref[k, :, 0:NB] = left[k, :, mycol]

        return carry

    lax.fori_loop(0, 8, below, 0)

    toprow = pl.ds(pl.multiple_of(NB * jnp.minimum(r, 3), NB), NB)

    @pl.when(r < 4)
    def _():
        out_ref[0] = ux[toprow, :]

        @pl.when(q < 4)
        def _():
            out_ref[0, :, 0:NB] = tx[toprow, mycol]

    @pl.when(gives)
    def _():
        scatter_raw(0).wait_send()
        top_piece(0).wait_send()

    @pl.when(q < 4)
    def _():
        for t in range(1, 8):
            scatter_raw(t).wait_send()
            top_piece(t).wait_send()

    @pl.when(r < 4)
    def _():
        mirror().wait_send()
        for off in range(1, NZ):
            old_slice(off).wait_send()

    for off in range(1, NZ):
        top_slice(off).wait_send()
    for h in range(2):
        for way in range(2):
            for k in range(4 - way):
                rs_send(h, way, k).wait_send()
                zag(*top_z, h, way, k).wait_send()
                zag(*old_z, h, way, k).wait_send()
    ring_raw.drain()
    ring_top.drain()


def local(matrix, pivots, lower_inverse, upper_inverse):
    a = matrix.reshape(8, NB, COLS)
    vm = pl.BlockSpec(memory_space=pltpu.VMEM)
    dma = pltpu.SemaphoreType.DMA
    out = pl.pallas_call(
        kernel,
        out_shape=jax.ShapeDtypeStruct((8, NB, COLS), BF),
        in_specs=[vm] * 4,
        out_specs=vm,
        scratch_shapes=[
            pltpu.VMEM((TOP, 128), F32),
            pltpu.VMEM((8, 1, 128), F32),
            pltpu.VMEM((8, 128, COLS), BF),
            pltpu.VMEM((2, 4, 128, NB), BF),
            pltpu.VMEM((2, 3, 128, NB), BF),
            pltpu.VMEM((8, 128, COLS), BF),
            pltpu.VMEM((4, NB, COLS), BF),
            pltpu.VMEM((12, NB, TOP), BF),
            pltpu.VMEM((8, 128, TOP), BF),
            pltpu.VMEM((8, NB, TOP), BF),
            pltpu.VMEM((TOP, TOP), BF),
            pltpu.VMEM((TOP, COLS), BF),
            dma((14,)), dma((14,)), dma((14,)), dma((14,)), dma((14,)), dma((14,)),
            dma((8,)), dma((1,)), dma((1,)), dma((1,)), dma((4,)), dma((7,)), dma((4,)),
            dma((8,)), dma((1,)), dma((7,)), dma((8,)),
            dma((32,)), dma((32,)), dma((16,)), dma((16,)),
        ],
        compiler_params=pltpu.CompilerParams(
            collective_id=0, has_side_effects=True, vmem_limit_bytes=60 * 1024 * 1024),
    )(a, pivots, lower_inverse, upper_inverse)
    return out.reshape(matrix.shape)


def solution(mesh):
    placed = (P(None, "prow", None, "pcol"), P(), P(), P())
    return jax.shard_map(
        local, mesh=mesh, in_specs=placed, out_specs=P(None, "prow", None, "pcol"), check_vma=False
    )
```

time: 983 us -> 101 us (0.10)
  waiting for transfers between devices: 883 us -> 0 us
  Pallas kernels: 0 us -> 91.7 us
  other arithmetic: 38.6 us -> 0 us
  local copies, waits for them, and re-layouts: 29.8 us -> 8.33 us
  matrix products: 16 us -> 0 us
  between operations: 13.9 us -> 0.01 us
    psum x8 -> x0, waiting for transfers between devices: 732 us -> none  [spread(): return lax.psum(kept, axis)]
    all_gather x4 -> x0, waiting for transfers between devices: 151 us -> none  [local(): gathered = lax.all_gather(picked, 'prow', axis=0, tiled=True)]
    pallas_call x0 -> x1, Pallas kernels: none -> 91.7 us  [local(): pl.pallas_call(kernel, out_shape=jax.ShapeDtypeStruct((8, NB, COLS), BF),...]
    select_n x14 -> x0, other arithmetic: 16.7 us -> none  [the longest x8 12.4 us: spread(): jnp.where(lax.axis_index(axis) == source, value, 0).astype(value.dtype)]
    scatter x4 -> x0, local copies, waits for them, and re-layouts: 16.6 us -> none  [local(): matrix_loc.at[jnp.where(moved_rows, chosen_local, local_rows)]]
    dot_general x12 -> x0, matrix products: 16 us -> none  [the longest x4 8.51 us: local(): jnp.dot(left_use, upper_use, preferred_element_type=jnp.float32)]
    scatter x9 -> x0, other arithmetic: 13.4 us -> none  [the longest x4 9.75 us: local(): matrix_loc.at[:, panel_local:panel_local + block_size].set(panel_put)]
  transfers between devices with their start and end apart: 12 -> 0, of which waited for: 12 -> 0; matrix products, arithmetic and copies ran while one was open for 3% -> 0% of each run, Pallas kernels for 0% -> 0%
where the time goes in v1:
time: 101 us; the launch traced here: 100 us
  Pallas kernels  91.7 us (91%)
  local copies, waits for them, and re-layouts  8.33 us (8%)
    pallas_call x1, Pallas kernels, local(): pl.pallas_call(kernel, out_shape=jax.ShapeDtypeStruct((8, NB, COLS), BF),...  91.7 us
    reshape x1, local copies, waits for them, and re-layouts, local(): a = matrix.reshape(8, NB, COLS)  4.37 us
    reshape x1, local copies, waits for them, and re-layouts, local(): return out.reshape(matrix.shape)  3.96 us

profile of v1, /device:TPU:1, one launch (start us, length us, event | category | flops | bytes accessed | tf_op | source)
XLA Modules:
  0.0 100.1 jit_solution(13227120452289618173)
XLA Ops:
  0.0 4.4 %reshape.6.a_ref = bf16[8,256,512]{2,1,0:T(8,128)(2,1)} reshape(bf16[8,256,2,256]{3,2,1,0:T(2,128)(2,1)} %param.4) | data formatting | bytes 4194304 | tf_op jit(solution)/shard_map/reshape | solution.py:594
  4.4 91.7 %shard_map.46 = bf16[8,256,512]{2,1,0:T(8,128)(2,1)} custom-call(bf16[8,256,512]{2,1,0:T(8,128)(2,1)} %reshape.6.a_ref, s32[4,256]{1,0:T(4,128)} %piv_ref.1, bf16[4,256,256]{2,1,0:T(8,128)(2,1)} %linv_ref.1, bf16[4,256,256]{2,1,0:T(8,128)(2,1)} %uinv_ref.1), custom_call_target="tpu_custom_call" | custom-call | tf_op jit(solution)/shard_map/pallas_call | solution.py:597
  96.1 4.0 %reshape.7 = bf16[8,256,2,256]{3,2,1,0:T(2,128)(2,1)} reshape(bf16[8,256,512]{2,1,0:T(8,128)(2,1)} %shard_map.46) | data formatting | bytes 4194304 | tf_op jit(solution)/shard_map/reshape | solution.py:623

commit v2 on v1

--- a/solution.py
+++ b/solution.py
@@ -19,10 +19,10 @@
 
 def kernel(a_ref, piv_ref, linv_ref, uinv_ref, out_ref,
            srcb, destr, contrib, rs_long, rs_short, top_own, old_own, pan, top_pan,
-           left, tx, ux,
+           left, tx, ux, pick, place, moved, piece_own, piece_rx,
            sem_rs, rem_rs, sem_tz, rem_tz, sem_dz, rem_dz,
            sem_sc, rem_sc, sem_mir, rem_mir, loc_sem, sem_ds, rem_ds,
-           sem_ts, rem_ts, sem_tsl, rem_tsl,
+           sem_ts, rem_ts, sem_px, rem_px, sem_tsl, rem_tsl,
            sem_ring, rem_ring, sem_par, rem_par):
     r = lax.axis_index("prow")
     q = lax.axis_index("pcol")
@@ -129,29 +129,45 @@
     def _():
         pl.semaphore_wait(barrier, 13)
 
-    def scatter_raw(t):
-        tx_, tc = t % 4, t // 4
-        return rcopy(a_ref.at[:, pl.ds(32 * t, 32), pl.ds(0, NB)],
-                     pan.at[pl.ds(0, 8), pl.ds(32 * t, 32), pl.ds(pl.multiple_of(NB * q, NB), NB)],
-                     sem_sc.at[t], rem_sc.at[0], dev(r, at_q(tx_, home_y, tc)))
-
-    def raw_self():
-        return pltpu.make_async_copy(a_ref.at[:, pl.ds(0, 32), pl.ds(0, NB)],
-                                     pan.at[pl.ds(0, 8), pl.ds(0, 32), pl.ds(pl.multiple_of(NB * q, NB), NB)],
-                                     loc_sem.at[0])
-
-    @pl.when(keeps)
-    def _():
-        raw_self().start()
-
-    @pl.when(gives)
-    def _():
-        scatter_raw(0).start()
-
-    @pl.when(q < 4)
-    def _():
-        for t in range(1, 8):
-            scatter_raw(t).start()
+    groups = ((0, 2), (2, 4), (6, 2))
+
+    def scatter_raw(t, n):
+        lo, size = groups[n]
+        return rcopy(a_ref.at[pl.ds(lo, size), pl.ds(32 * t, 32), pl.ds(0, NB)],
+                     pan.at[pl.ds(lo, size), pl.ds(32 * t, 32), pl.ds(pl.multiple_of(NB * q, NB), NB)],
+                     sem_sc.at[8 * n + t], rem_sc.at[n], dev(r, at_q(t % 4, home_y, t // 4)))
+
+    def raw_self(n):
+        lo, size = groups[n]
+        return pltpu.make_async_copy(
+            a_ref.at[pl.ds(lo, size), pl.ds(0, 32), pl.ds(0, NB)],
+            pan.at[pl.ds(lo, size), pl.ds(0, 32), pl.ds(pl.multiple_of(NB * q, NB), NB)],
+            loc_sem.at[3 + n])
+
+    def raw_start(n):
+        @pl.when(keeps)
+        def _():
+            raw_self(n).start()
+
+        @pl.when(gives)
+        def _():
+            scatter_raw(0, n).start()
+
+        @pl.when(q < 4)
+        def _():
+            for t in range(1, 8):
+                scatter_raw(t, n).start()
+
+    def raw_wait(n):
+        lo, size = groups[n]
+
+        @pl.when(keeps)
+        def _():
+            raw_self(n).wait()
+
+        @pl.when(jnp.logical_not(keeps))
+        def _():
+            got(pan.at[pl.ds(lo, size), mine32, minec], sem_sc.at[0], rem_sc.at[n], dev(r, mate))
 
     def mirror():
         return rcopy(a_ref.at[0, pl.ds(128, 128), :],
@@ -162,22 +178,18 @@
         return pltpu.make_async_copy(a_ref.at[0, pl.ds(0, 128), :],
                                      old_own.at[r % 4, pl.ds(0, 128), :], loc_sem.at[1])
 
-    @pl.when(r < 4)
-    def _():
-        mirror().start()
-        old_self().start()
-
-    def contribute(i, carry):
-        off = 4 + (i % 2) * ((i + 1) // 2) - (1 - i % 2) * (i // 2)
-        chunk = (r + off) % NZ
-        want = srcb[pl.ds(pl.multiple_of(chunk * 128, 128), 128), :]
-        tiles = []
-        for t in range(16):
-            gid = lane + ((t // 2 * NZ + r) * NB + (t % 2) * 128).astype(F32)
-            tiles.append(jnp.where(want == gid, 1.0, 0.0).astype(BF))
-        pick = jnp.concatenate(tiles, axis=1)
-        contrib[chunk] = dot(pick, a_ref[...].reshape(2048, COLS)).astype(BF)
-        return carry
+    def contribute(h):
+        def body(c, carry):
+            if h == 0:
+                want = srcb[pl.ds(pl.multiple_of(c * 128, 128), 128), :]
+                for t in range(16):
+                    gid = lane + ((t // 2 * NZ + r) * NB + (t % 2) * 128).astype(F32)
+                    pick[c, :, 128 * t:128 * (t + 1)] = jnp.where(want == gid, 1.0, 0.0).astype(BF)
+            contrib[c, :, NB * h:NB * (h + 1)] = dot(
+                pick[c], a_ref[:, :, NB * h:NB * (h + 1)].reshape(2048, NB)).astype(BF)
+            return carry
+
+        lax.fori_loop(0, 8, body, 0)
 
     def half(h):
         return pl.ds(NB * h, NB)
@@ -315,8 +327,8 @@
                                pl.ds(pl.multiple_of(4 * rows * oc, 4 * rows), 4 * rows),
                                pl.ds(pl.multiple_of(NB * panel_of(j), NB), NB)]
 
-        def start(self, stage):
-            for part in range(2):
+        def start(self, stage, parts=(0, 1)):
+            for part in parts:
                 self.copy(part, stage, 0).start()
                 self.copy(part, stage, 1).start()
 
@@ -362,57 +374,125 @@
 
     def old_slice_self():
         return pltpu.make_async_copy(pan.at[0, mine32, minec], pan.at[8 + r % 4, mine32, minec],
-                                     loc_sem.at[2])
+                                     loc_sem.at[0])
 
     def top_piece(t):
-        return rcopy(top_own.at[r, pl.ds(16 * t, 16), pl.ds(0, NB)],
-                     top_pan.at[r, pl.ds(16 * t, 16), pl.ds(pl.multiple_of(NB * q, NB), NB)],
+        return rcopy(contrib.at[:, pl.ds(16 * t, 16), pl.ds(0, NB)], piece_own,
                      sem_ts.at[t], rem_ts.at[0], dev(r, at_q(t % 4, home_y, t // 4)))
 
     def top_piece_self():
-        return pltpu.make_async_copy(top_own.at[r, pl.ds(0, 16), pl.ds(0, NB)],
-                                     top_pan.at[r, pl.ds(0, 16), pl.ds(pl.multiple_of(NB * q, NB), NB)],
-                                     loc_sem.at[3])
+        return pltpu.make_async_copy(contrib.at[:, pl.ds(0, 16), pl.ds(0, NB)], piece_own, loc_sem.at[2])
+
+    def piece_home(off):
+        return rcopy(piece_own.at[plane(off)], piece_rx.at[r], sem_px.at[off - 1], rem_px.at[r],
+                     dev(plane(off), q))
 
     def top_slice(off):
         v = top_pan.at[r, mine16, minec]
         return rcopy(v, v, sem_tsl.at[off - 1], rem_tsl.at[r], dev(plane(off), q))
 
-    lax.fori_loop(0, 3, contribute, 0)
-    for h in range(2):
-        rs_send(h, 0, 0).start()
-        rs_send(h, 1, 0).start()
-    lax.fori_loop(3, 8, contribute, 0)
-
-    for h in range(2):
-        rs_step(h, 0, 1)
-        rs_step(h, 1, 1)
+    row_id = lax.broadcasted_iota(jnp.int32, (NB, 1), 0).astype(F32)
+
+    def displaced_own(k, carry):
+        mine = row_id + ((k * NZ + r) * NB).astype(F32)
+        seen = None
+        for t in range(8):
+            hit = jnp.where(destr[t] == mine, 1.0, 0.0)
+            seen = hit if seen is None else seen + hit
+            place[k, :, 128 * t:128 * (t + 1)] = hit.astype(BF)
+        some = jnp.sum(seen, axis=1, keepdims=True)
+        moved[k] = jnp.broadcast_to(some, (NB, 128))
+        rows = dot(place[k], old_own[...].reshape(TOP, COLS))
+        out_ref[k] = jnp.where(some > 0.5, rows, a_ref[k].astype(F32)).astype(BF)
+        return carry
+
+    def displaced_panel(k, carry):
+        rows = dot(place[k], pan[8:12].reshape(TOP, TOP))
+        left[k] = jnp.where(moved[k][:, 0:1] > 0.5, rows, pan[k].astype(F32)).astype(BF)
+        return carry
+
+    raw_start(0)
+
+    @pl.when(r < 4)
+    def _():
+        mirror().start()
+        old_self().start()
+
+    contribute(0)
 
     @pl.when(keeps)
     def _():
-        raw_self().wait()
-
-    @pl.when(jnp.logical_not(keeps))
-    def _():
-        got(pan.at[pl.ds(0, 8), mine32, minec], sem_sc.at[0], rem_sc.at[0], dev(r, mate))
+        top_piece_self().start()
+
+    @pl.when(gives)
+    def _():
+        top_piece(0).start()
+
+    @pl.when(q < 4)
+    def _():
+        for t in range(1, 8):
+            top_piece(t).start()
+
+    rs_send(0, 0, 0).start()
+    rs_send(0, 1, 0).start()
+    raw_start(1)
+    raw_start(2)
+    contribute(1)
+    rs_send(1, 0, 0).start()
+    rs_send(1, 1, 0).start()
+
+    @pl.when(r < 4)
+    def _():
+        old_self().wait()
+
+    @pl.when(r >= 4)
+    def _():
+        got(old_own.at[(7 - r) % 4, pl.ds(128, 128), :], sem_mir.at[0], rem_mir.at[0], dev(7 - r, q))
+
+    for h in range(2):
+        zag_step(*old_z, h, 0)
+
+    raw_wait(0)
 
     @pl.when(r < 4)
     def _():
         old_slice_self().start()
         for off in range(1, NZ):
             old_slice(off).start()
-        old_self().wait()
-
-    @pl.when(r >= 4)
-    def _():
-        got(old_own.at[(7 - r) % 4, pl.ds(128, 128), :], sem_mir.at[0], rem_mir.at[0], dev(7 - r, q))
+
+    for h in range(2):
+        rs_step(h, 0, 1)
+        rs_step(h, 1, 1)
+
+    @pl.when(keeps)
+    def _():
+        top_piece_self().wait()
+
+    @pl.when(jnp.logical_not(keeps))
+    def _():
+        got(piece_own, sem_ts.at[0], rem_ts.at[0], dev(r, mate))
+
+    for off in range(1, NZ):
+        piece_home(off).start()
+
+    for h in range(2):
+        zag_step(*old_z, h, 1)
 
     for h in range(2):
         rs_step(h, 0, 2)
         rs_step(h, 1, 2)
 
-    for h in range(2):
-        zag_step(*old_z, h, 0)
+    total = piece_own[r]
+    for off in range(1, NZ):
+        src = plane(off)
+        got(piece_rx.at[src], sem_px.at[0], rem_px.at[src], dev(r, mate))
+        total = total + piece_rx[src]
+    top_pan[r, mine16, minec] = total
+    for off in range(1, NZ):
+        top_slice(off).start()
+
+    raw_wait(1)
+    ring_raw.start(0, (0,))
 
     for a in range(4):
         @pl.when(r != a)
@@ -423,49 +503,11 @@
     def _():
         old_slice_self().wait()
 
-    ring_raw.start(0)
+    raw_wait(2)
+    ring_raw.start(0, (1,))
 
     for h in range(2):
         rs_step(h, 0, 3)
-
-    rs_end(0)
-
-    @pl.when(keeps)
-    def _():
-        top_piece_self().start()
-
-    @pl.when(gives)
-    def _():
-        top_piece(0).start()
-
-    @pl.when(q < 4)
-    def _():
-        for t in range(1, 8):
-            top_piece(t).start()
-
-    zag_step(*top_z, 0, 0)
-    rs_end(1)
-    zag_step(*top_z, 1, 0)
-
-    for h in range(2):
-        zag_step(*old_z, h, 1)
-
-    ring_raw.forward(0)
-
-    @pl.when(keeps)
-    def _():
-        top_piece_self().wait()
-
-    @pl.when(jnp.logical_not(keeps))
-    def _():
-        got(top_pan.at[r, mine16, minec], sem_ts.at[0], rem_ts.at[0], dev(r, mate))
-
-    for off in range(1, NZ):
-        top_slice(off).start()
-
-    for h in range(2):
-        zag_step(*top_z, h, 1)
-    for h in range(2):
         zag_step(*old_z, h, 2)
 
     for off in range(1, NZ):
@@ -473,48 +515,41 @@
         got(top_pan.at[src, mine16, minec], sem_tsl.at[0], rem_tsl.at[src], dev(r, mate))
 
     ring_top.start(0)
+
+    for h in range(2):
+        rs_end(h)
+        zag_step(*top_z, h, 0)
+    for h in range(2):
+        zag_step(*old_z, h, 3)
+
+    ring_raw.forward(0)
+    ring_top.forward(0)
+    for h in range(2):
+        zag_step(*top_z, h, 1)
+
     ring_raw.finish(0)
     ring_raw.start(1)
-
-    for h in range(2):
-        zag_step(*top_z, h, 2)
-    for h in range(2):
-        zag_step(*old_z, h, 3)
-
-    ring_top.forward(0)
     ring_top.finish(0)
     ring_top.start(1)
 
     for h in range(2):
-        zag_step(*top_z, h, 3)
+        zag_end(*old_z, h)
+    for h in range(2):
+        zag_step(*top_z, h, 2)
+
+    lax.fori_loop(0, 8, displaced_own, 0)
 
     ring_raw.forward(1)
     ring_top.forward(1)
     for h in range(2):
-        zag_end(*old_z, h)
-        zag_end(*top_z, h)
+        zag_step(*top_z, h, 3)
+
     ring_raw.finish(1)
     ring_raw.close()
-
-    row_id = lax.broadcasted_iota(jnp.int32, (NB, 1), 0).astype(F32)
-
-    def displaced(k, carry):
-        mine = row_id + ((k * NZ + r) * NB).astype(F32)
-        tiles, seen = [], None
-        for t in range(8):
-            hit = jnp.where(destr[t] == mine, 1.0, 0.0)
-            seen = hit if seen is None else seen + hit
-            tiles.append(hit.astype(BF))
-        pick = jnp.concatenate(tiles, axis=1)
-        moved = jnp.sum(seen, axis=1, keepdims=True) > 0.5
-        rows = dot(pick, pan[8:12].reshape(TOP, TOP))
-        left[k] = jnp.where(moved, rows, pan[k].astype(F32)).astype(BF)
-        rows = dot(pick, old_own[...].reshape(TOP, COLS))
-        out_ref[k] = jnp.where(moved, rows, a_ref[k].astype(F32)).astype(BF)
-        return carry
-
-    lax.fori_loop(0, 8, displaced, 0)
-
+    lax.fori_loop(0, 8, displaced_panel, 0)
+
+    for h in range(2):
+        zag_end(*top_z, h)
     ring_top.finish(1)
     ring_top.close()
 
@@ -534,22 +569,29 @@
 
     mycol = pl.ds(pl.multiple_of(NB * jnp.minimum(q, 3), NB), NB)
 
-    def below(k, carry):
+    TWO = 2
+
+    def below(i, carry):
+        ks = pl.ds(TWO * i, TWO)
+        m = TWO * NB
         for s in range(4):
             b, e = s * NB, (s + 1) * NB
-            l_row = dot(left[k, :, b:e], uinv_ref[s]).astype(BF)
-            left[k, :, b:e] = l_row
+            l_row = dot(left[ks, :, b:e].reshape(m, NB), uinv_ref[s]).astype(BF)
+            left[ks, :, b:e] = l_row.reshape(TWO, NB, NB)
             if s < 3:
-                left[k, :, e:] = (left[k, :, e:].astype(F32) - dot(l_row, tx[b:e, e:])).astype(BF)
-        out_ref[k] = (out_ref[k].astype(F32) - dot(left[k], ux[...])).astype(BF)
+                rest = left[ks, :, e:].reshape(m, TOP - e).astype(F32)
+                left[ks, :, e:] = (rest - dot(l_row, tx[b:e, e:])).astype(BF).reshape(TWO, NB, TOP - e)
+        rest = out_ref[ks].reshape(m, COLS).astype(F32)
+        rest = rest - dot(left[ks].reshape(m, TOP), ux[...])
+        out_ref[ks] = rest.astype(BF).reshape(TWO, NB, COLS)
 
         @pl.when(q < 4)
         def _():
-            out_ref[k, :, 0:NB] = left[k, :, mycol]
+            out_ref[ks, :, 0:NB] = left[ks, :, mycol]
 
         return carry
 
-    lax.fori_loop(0, 8, below, 0)
+    lax.fori_loop(0, 8 // TWO, below, 0)
 
     toprow = pl.ds(pl.multiple_of(NB * jnp.minimum(r, 3), NB), NB)
 
@@ -563,13 +605,15 @@
 
     @pl.when(gives)
     def _():
-        scatter_raw(0).wait_send()
+        for n in range(3):
+            scatter_raw(0, n).wait_send()
         top_piece(0).wait_send()
 
     @pl.when(q < 4)
     def _():
         for t in range(1, 8):
-            scatter_raw(t).wait_send()
+            for n in range(3):
+                scatter_raw(t, n).wait_send()
             top_piece(t).wait_send()
 
     @pl.when(r < 4)
@@ -578,6 +622,8 @@
         for off in range(1, NZ):
             old_slice(off).wait_send()
 
+    for off in range(1, NZ):
+        piece_home(off).wait_send()
     for off in range(1, NZ):
         top_slice(off).wait_send()
     for h in range(2):
@@ -591,7 +637,8 @@
 
 
 def local(matrix, pivots, lower_inverse, upper_inverse):
-    a = matrix.reshape(8, NB, COLS)
+    rows = matrix.reshape(256, 8, 2, NB).transpose(0, 2, 1, 3)
+    a = lax.optimization_barrier(rows).transpose(0, 2, 1, 3).reshape(8, NB, COLS)
     vm = pl.BlockSpec(memory_space=pltpu.VMEM)
     dma = pltpu.SemaphoreType.DMA
     out = pl.pallas_call(
@@ -612,13 +659,18 @@
             pltpu.VMEM((8, NB, TOP), BF),
             pltpu.VMEM((TOP, TOP), BF),
             pltpu.VMEM((TOP, COLS), BF),
+            pltpu.VMEM((8, 128, 2048), BF),
+            pltpu.VMEM((8, NB, TOP), BF),
+            pltpu.VMEM((8, NB, 128), F32),
+            pltpu.VMEM((8, 16, NB), BF),
+            pltpu.VMEM((8, 16, NB), BF),
             dma((14,)), dma((14,)), dma((14,)), dma((14,)), dma((14,)), dma((14,)),
-            dma((8,)), dma((1,)), dma((1,)), dma((1,)), dma((4,)), dma((7,)), dma((4,)),
-            dma((8,)), dma((1,)), dma((7,)), dma((8,)),
+            dma((24,)), dma((3,)), dma((1,)), dma((1,)), dma((6,)), dma((7,)), dma((4,)),
+            dma((8,)), dma((1,)), dma((7,)), dma((8,)), dma((7,)), dma((8,)),
             dma((32,)), dma((32,)), dma((16,)), dma((16,)),
         ],
         compiler_params=pltpu.CompilerParams(
-            collective_id=0, has_side_effects=True, vmem_limit_bytes=60 * 1024 * 1024),
+            collective_id=0, has_side_effects=True, vmem_limit_bytes=46 * 1024 * 1024),
     )(a, pivots, lower_inverse, upper_inverse)
     return out.reshape(matrix.shape)
 

time: 101 us -> 86 us (0.85)
  Pallas kernels: 91.7 us -> 81.7 us
  local copies, waits for them, and re-layouts: 8.33 us -> 4.16 us
    pallas_call x1, Pallas kernels: 91.7 us -> 81.7 us  [local(): pl.pallas_call(kernel, out_shape=jax.ShapeDtypeStruct((8, NB, COLS), BF),...]
    reshape x1, local copies, waits for them, and re-layouts: 4.37 us -> 2.12 us  [local(): rows = matrix.reshape(256, 8, 2, NB).transpose(0, 2, 1, 3)]
    reshape x1, local copies, waits for them, and re-layouts: 3.96 us -> 2.03 us  [local(): return out.reshape(matrix.shape)]
where the time goes in v2:
time: 86 us
  Pallas kernels  81.7 us (95%)
  local copies, waits for them, and re-layouts  4.16 us (5%)
    pallas_call x1, Pallas kernels, local(): pl.pallas_call(kernel, out_shape=jax.ShapeDtypeStruct((8, NB, COLS), BF),...  81.7 us
    reshape x1, local copies, waits for them, and re-layouts, local(): rows = matrix.reshape(256, 8, 2, NB).transpose(0, 2, 1, 3)  2.12 us
    reshape x1, local copies, waits for them, and re-layouts, local(): return out.reshape(matrix.shape)  2.03 us

profile of v2, /device:TPU:1, one launch (start us, length us, event | category | flops | bytes accessed | tf_op | source)
XLA Modules:
  0.0 86.0 jit_solution(4693835067151982438)
XLA Ops:
  0.0 0.0 copy-start
  0.0 0.0 copy-start.1
  0.0 0.0 copy-start.2
  0.0 2.1 %copy.7 = bf16[256,8,2,256]{3,1,2,0:T(8,128)(2,1)S(1)} copy(bf16[256,8,2,256]{3,2,1,0:T(2,128)(2,1)} %bitcast.8) | data formatting | bytes 4194304 | tf_op jit(solution)/shard_map/reshape | solution.py:640
  2.1 0.0 copy-done
  2.1 0.0 copy-done.1
  2.2 0.0 copy-done.2
  2.2 81.7 %shard_map.46 = bf16[8,256,512]{2,1,0:T(8,128)(2,1)S(1)} custom-call(bf16[8,256,512]{2,1,0:T(8,128)(2,1)S(1)} %bitcast.7, s32[4,256]{1,0:T(4,128)S(1)} %copy-done.2, bf16[4,256,256]{2,1,0:T(8,128)(2,1)S(1)} %copy-done, bf16[4,256,256]{2,1,0:T(8,128)(2,1)S(1)} %copy-done.1), custom_call_target="tpu_custom_call" | custom-call | tf_op jit(solution)/shard_map/pallas_call | solution.py:644
  83.9 2.0 %reshape.11 = bf16[8,256,2,256]{3,2,1,0:T(2,128)(2,1)} reshape(bf16[8,256,512]{2,1,0:T(8,128)(2,1)S(1)} %shard_map.46) | data formatting | bytes 4194304 | tf_op jit(solution)/shard_map/reshape | solution.py:675
Async XLA Ops:
  0.0 2.1 %copy-start = (bf16[4,256,256]{2,1,0:T(8,128)(2,1)S(1)}, bf16[4,256,256]{2,1,0:T(8,128)(2,1)}, u32[]{:S(2)}) copy-start(bf16[4,256,256]{2,1,0:T(8,128)(2,1)} %linv_ref.1) | copy-start | bytes 1572868
  0.0 2.1 %copy-start.1 = (bf16[4,256,256]{2,1,0:T(8,128)(2,1)S(1)}, bf16[4,256,256]{2,1,0:T(8,128)(2,1)}, u32[]{:S(2)}) copy-start(bf16[4,256,256]{2,1,0:T(8,128)(2,1)} %uinv_ref.1) | copy-start | bytes 1572868
  0.0 2.2 %copy-start.2 = (s32[4,256]{1,0:T(4,128)S(1)}, s32[4,256]{1,0:T(4,128)}, u32[]{:S(2)}) copy-start(s32[4,256]{1,0:T(4,128)} %piv_ref.1) | copy-start | bytes 12292

commit v3 on v2

--- a/solution.py
+++ b/solution.py
@@ -13,16 +13,19 @@
 COLS = 512
 
 
+ORDER = ('w0', 'w1', 'w2', 'os', 'C0', 'r00', 'C1', 'r10', 'g0', 'ls', 'r01', 'g1', 'R00s', 'P', 'r11', 'lg', 'O00s', 'O10s', 'R00f', 'r02', 'r12', 'g2', 'R10s', 'R00e', 'O00f', 'O10f', 'r03', 'r13', 'R10f', 're0', 'ps', 're1', 'O00e', 'O10e', 'O01s', 'O11s', 'R10e', 'R01s', 'R11s', 'ph', 't00', 't10', 'og', 'd00', 'd10', 'O01f', 'O11f', 'sg', 'S00s', 'S10s', 't01', 't11', 'd01', 'd11', 'O01e', 'O11e', 'O0c', 'O1c', 'Y0', 'S00f', 'S10f', 'R01f', 'R11f', 't02', 't12', 'd02', 'd12', 'S00e', 'S10e', 'S01s', 'S11s', 'R01e', 'R11e', 't03', 't13', 'Y1', 'S01f', 'S11f', 'd03', 'd13', 'S01e', 'S11e', 'R0c', 'R1c', 'S0c', 'S1c', 'K', 'L', 'de0', 'de1', 'X', 'te0', 'te1', 'U', 'F')
+
+
 def dot(a, b):
     return jnp.dot(a, b, preferred_element_type=F32)
 
 
 def kernel(a_ref, piv_ref, linv_ref, uinv_ref, out_ref,
            srcb, destr, contrib, rs_long, rs_short, top_own, old_own, pan, top_pan,
-           left, tx, ux, pick, place, moved, piece_own, piece_rx,
+           left, tx, ux, pick, place, moved,
            sem_rs, rem_rs, sem_tz, rem_tz, sem_dz, rem_dz,
            sem_sc, rem_sc, sem_mir, rem_mir, loc_sem, sem_ds, rem_ds,
-           sem_ts, rem_ts, sem_px, rem_px, sem_tsl, rem_tsl,
+           sem_ts, rem_ts, sem_tsl, rem_tsl,
            sem_ring, rem_ring, sem_par, rem_par):
     r = lax.axis_index("prow")
     q = lax.axis_index("pcol")
@@ -129,7 +132,7 @@
     def _():
         pl.semaphore_wait(barrier, 13)
 
-    groups = ((0, 2), (2, 4), (6, 2))
+    groups = ((0, 1), (1, 3), (4, 4))
 
     def scatter_raw(t, n):
         lo, size = groups[n]
@@ -179,17 +182,20 @@
                                      old_own.at[r % 4, pl.ds(0, 128), :], loc_sem.at[1])
 
     def contribute(h):
-        def body(c, carry):
+        def body(i, carry):
+            cs = pl.ds(4 * i, 4)
             if h == 0:
-                want = srcb[pl.ds(pl.multiple_of(c * 128, 128), 128), :]
-                for t in range(16):
-                    gid = lane + ((t // 2 * NZ + r) * NB + (t % 2) * 128).astype(F32)
-                    pick[c, :, 128 * t:128 * (t + 1)] = jnp.where(want == gid, 1.0, 0.0).astype(BF)
-            contrib[c, :, NB * h:NB * (h + 1)] = dot(
-                pick[c], a_ref[:, :, NB * h:NB * (h + 1)].reshape(2048, NB)).astype(BF)
+                for j in range(4):
+                    c = 4 * i + j
+                    want = srcb[pl.ds(pl.multiple_of(c * 128, 128), 128), :]
+                    for t in range(16):
+                        gid = lane + ((t // 2 * NZ + r) * NB + (t % 2) * 128).astype(F32)
+                        pick[c, :, 128 * t:128 * (t + 1)] = jnp.where(want == gid, 1.0, 0.0).astype(BF)
+            rows = dot(pick[cs].reshape(512, 2048), a_ref[:, :, NB * h:NB * (h + 1)].reshape(2048, NB))
+            contrib[cs, :, NB * h:NB * (h + 1)] = rows.astype(BF).reshape(4, 128, NB)
             return carry
 
-        lax.fori_loop(0, 8, body, 0)
+        lax.fori_loop(0, 2, body, 0)
 
     def half(h):
         return pl.ds(NB * h, NB)
@@ -253,8 +259,8 @@
     old_z = (old_view, sem_dz, rem_dz)
 
     class Ring:
-        def __init__(self, buf, n0, rows, base):
-            self.buf, self.n0, self.rows, self.base = buf, n0, rows, base
+        def __init__(self, buf, first, n0, rows, base):
+            self.buf, self.first, self.n0, self.rows, self.base = buf, first, n0, rows, base
 
         def reg(self, part, stage, j, piece=None):
             n0, rows = self.n0, self.rows
@@ -262,7 +268,7 @@
             if piece is not None:
                 n = n // 2
                 lo = lo + n * piece
-            k = pl.ds(lo, n)
+            k = pl.ds(self.first + lo, n)
             along_y = (part == 0) == (stage == 0)
             if stage == 0:
                 col = panel_of(j) if along_y else p
@@ -322,36 +328,32 @@
             oc = 1 - core
             if part == 0:
                 gg = oc * 4 + j
-                return self.buf.at[pl.ds(0, n0 // 2), pl.ds(pl.multiple_of(rows * gg, rows), rows), :]
-            return self.buf.at[pl.ds(n0 // 2, n0 // 2),
+                return self.buf.at[pl.ds(self.first, n0 // 2), pl.ds(pl.multiple_of(rows * gg, rows), rows), :]
+            return self.buf.at[pl.ds(self.first + n0 // 2, n0 // 2),
                                pl.ds(pl.multiple_of(4 * rows * oc, 4 * rows), 4 * rows),
                                pl.ds(pl.multiple_of(NB * panel_of(j), NB), NB)]
 
-        def start(self, stage, parts=(0, 1)):
-            for part in parts:
-                self.copy(part, stage, 0).start()
-                self.copy(part, stage, 1).start()
-
-        def forward(self, stage):
-            for part in range(2):
-                self.wait(part, stage, 0)
-                self.copy(part, stage, 2).start()
-                self.wait(part, stage, 1)
-                self.copy(part, stage, 3).start()
-                if stage == 1:
-                    self.par(part, 1).start()
-                    self.par(part, 2).start()
-
-        def finish(self, stage):
-            for part in range(2):
-                self.wait(part, stage, 2)
-                self.wait(part, stage, 3)
-                self.par(part, 0 if stage == 0 else 3).start()
-
-        def close(self):
-            for part in range(2):
-                for piece in range(4):
-                    self.par_wait(part, piece)
+        def start(self, stage, part):
+            self.copy(part, stage, 0).start()
+            self.copy(part, stage, 1).start()
+
+        def forward(self, stage, part):
+            self.wait(part, stage, 0)
+            self.copy(part, stage, 2).start()
+            self.wait(part, stage, 1)
+            self.copy(part, stage, 3).start()
+            if stage == 1:
+                self.par(part, 1).start()
+                self.par(part, 2).start()
+
+        def finish(self, stage, part):
+            self.wait(part, stage, 2)
+            self.wait(part, stage, 3)
+            self.par(part, 0 if stage == 0 else 3).start()
+
+        def close(self, part):
+            for piece in range(4):
+                self.par_wait(part, piece)
 
         def drain(self):
             for part in range(2):
@@ -361,8 +363,9 @@
                 for piece in range(4):
                     self.par(part, piece).wait_send()
 
-    ring_raw = Ring(pan, 12, 32, 0)
-    ring_top = Ring(top_pan, 8, 16, 16)
+    ring_raw = Ring(pan, 0, 8, 32, 0)
+    ring_top = Ring(top_pan, 0, 8, 16, 16)
+    ring_old = Ring(pan, 8, 4, 32, 32)
 
     mine32 = pl.ds(pl.multiple_of(32 * g, 32), 32)
     mine16 = pl.ds(pl.multiple_of(16 * g, 16), 16)
@@ -377,15 +380,14 @@
                                      loc_sem.at[0])
 
     def top_piece(t):
-        return rcopy(contrib.at[:, pl.ds(16 * t, 16), pl.ds(0, NB)], piece_own,
+        return rcopy(top_own.at[r, pl.ds(16 * t, 16), pl.ds(0, NB)],
+                     top_pan.at[r, pl.ds(16 * t, 16), pl.ds(pl.multiple_of(NB * q, NB), NB)],
                      sem_ts.at[t], rem_ts.at[0], dev(r, at_q(t % 4, home_y, t // 4)))
 
     def top_piece_self():
-        return pltpu.make_async_copy(contrib.at[:, pl.ds(0, 16), pl.ds(0, NB)], piece_own, loc_sem.at[2])
-
-    def piece_home(off):
-        return rcopy(piece_own.at[plane(off)], piece_rx.at[r], sem_px.at[off - 1], rem_px.at[r],
-                     dev(plane(off), q))
+        return pltpu.make_async_copy(
+            top_own.at[r, pl.ds(0, 16), pl.ds(0, NB)],
+            top_pan.at[r, pl.ds(0, 16), pl.ds(pl.multiple_of(NB * q, NB), NB)], loc_sem.at[2])
 
     def top_slice(off):
         v = top_pan.at[r, mine16, minec]
@@ -393,187 +395,58 @@
 
     row_id = lax.broadcasted_iota(jnp.int32, (NB, 1), 0).astype(F32)
 
-    def displaced_own(k, carry):
+    def find_places(k, carry):
         mine = row_id + ((k * NZ + r) * NB).astype(F32)
         seen = None
         for t in range(8):
             hit = jnp.where(destr[t] == mine, 1.0, 0.0)
             seen = hit if seen is None else seen + hit
             place[k, :, 128 * t:128 * (t + 1)] = hit.astype(BF)
-        some = jnp.sum(seen, axis=1, keepdims=True)
-        moved[k] = jnp.broadcast_to(some, (NB, 128))
-        rows = dot(place[k], old_own[...].reshape(TOP, COLS))
-        out_ref[k] = jnp.where(some > 0.5, rows, a_ref[k].astype(F32)).astype(BF)
+        moved[k] = jnp.broadcast_to(jnp.sum(seen, axis=1, keepdims=True), (NB, 128))
         return carry
 
-    def displaced_panel(k, carry):
-        rows = dot(place[k], pan[8:12].reshape(TOP, TOP))
-        left[k] = jnp.where(moved[k][:, 0:1] > 0.5, rows, pan[k].astype(F32)).astype(BF)
+    def displaced_own(i, carry):
+        ks = pl.ds(2 * i, 2)
+        rows = dot(place[ks].reshape(512, TOP), old_own[...].reshape(TOP, COLS)).reshape(2, NB, COLS)
+        for j in range(2):
+            k = 2 * i + j
+            out_ref[k] = jnp.where(moved[k][:, 0:1] > 0.5, rows[j], a_ref[k].astype(F32)).astype(BF)
         return carry
 
-    raw_start(0)
-
-    @pl.when(r < 4)
-    def _():
-        mirror().start()
-        old_self().start()
-
-    contribute(0)
-
-    @pl.when(keeps)
-    def _():
-        top_piece_self().start()
-
-    @pl.when(gives)
-    def _():
-        top_piece(0).start()
-
-    @pl.when(q < 4)
-    def _():
-        for t in range(1, 8):
-            top_piece(t).start()
-
-    rs_send(0, 0, 0).start()
-    rs_send(0, 1, 0).start()
-    raw_start(1)
-    raw_start(2)
-    contribute(1)
-    rs_send(1, 0, 0).start()
-    rs_send(1, 1, 0).start()
-
-    @pl.when(r < 4)
-    def _():
-        old_self().wait()
-
-    @pl.when(r >= 4)
-    def _():
-        got(old_own.at[(7 - r) % 4, pl.ds(128, 128), :], sem_mir.at[0], rem_mir.at[0], dev(7 - r, q))
-
-    for h in range(2):
-        zag_step(*old_z, h, 0)
-
-    raw_wait(0)
-
-    @pl.when(r < 4)
-    def _():
-        old_slice_self().start()
-        for off in range(1, NZ):
-            old_slice(off).start()
-
-    for h in range(2):
-        rs_step(h, 0, 1)
-        rs_step(h, 1, 1)
-
-    @pl.when(keeps)
-    def _():
-        top_piece_self().wait()
-
-    @pl.when(jnp.logical_not(keeps))
-    def _():
-        got(piece_own, sem_ts.at[0], rem_ts.at[0], dev(r, mate))
-
-    for off in range(1, NZ):
-        piece_home(off).start()
-
-    for h in range(2):
-        zag_step(*old_z, h, 1)
-
-    for h in range(2):
-        rs_step(h, 0, 2)
-        rs_step(h, 1, 2)
-
-    total = piece_own[r]
-    for off in range(1, NZ):
-        src = plane(off)
-        got(piece_rx.at[src], sem_px.at[0], rem_px.at[src], dev(r, mate))
-        total = total + piece_rx[src]
-    top_pan[r, mine16, minec] = total
-    for off in range(1, NZ):
-        top_slice(off).start()
-
-    raw_wait(1)
-    ring_raw.start(0, (0,))
-
-    for a in range(4):
-        @pl.when(r != a)
-        def _():
-            got(pan.at[8 + a, mine32, minec], sem_ds.at[0], rem_ds.at[a], dev(r, mate))
-
-    @pl.when(r < 4)
-    def _():
-        old_slice_self().wait()
-
-    raw_wait(2)
-    ring_raw.start(0, (1,))
-
-    for h in range(2):
-        rs_step(h, 0, 3)
-        zag_step(*old_z, h, 2)
-
-    for off in range(1, NZ):
-        src = plane(off)
-        got(top_pan.at[src, mine16, minec], sem_tsl.at[0], rem_tsl.at[src], dev(r, mate))
-
-    ring_top.start(0)
-
-    for h in range(2):
-        rs_end(h)
-        zag_step(*top_z, h, 0)
-    for h in range(2):
-        zag_step(*old_z, h, 3)
-
-    ring_raw.forward(0)
-    ring_top.forward(0)
-    for h in range(2):
-        zag_step(*top_z, h, 1)
-
-    ring_raw.finish(0)
-    ring_raw.start(1)
-    ring_top.finish(0)
-    ring_top.start(1)
-
-    for h in range(2):
-        zag_end(*old_z, h)
-    for h in range(2):
-        zag_step(*top_z, h, 2)
-
-    lax.fori_loop(0, 8, displaced_own, 0)
-
-    ring_raw.forward(1)
-    ring_top.forward(1)
-    for h in range(2):
-        zag_step(*top_z, h, 3)
-
-    ring_raw.finish(1)
-    ring_raw.close()
-    lax.fori_loop(0, 8, displaced_panel, 0)
-
-    for h in range(2):
-        zag_end(*top_z, h)
-    ring_top.finish(1)
-    ring_top.close()
-
-    tx[...] = top_pan[...].reshape(TOP, TOP)
-    ux[...] = top_own[...].reshape(TOP, COLS)
-    for s in range(4):
-        b, e = s * NB, (s + 1) * NB
-        u_own = dot(linv_ref[s], ux[b:e, :]).astype(BF)
-        ux[b:e, :] = u_own
-        if s < 3:
+    def displaced_panel(i, carry):
+        ks = pl.ds(2 * i, 2)
+        rows = dot(place[ks].reshape(512, TOP), pan[8:12].reshape(TOP, TOP))
+        left[ks] = rows.astype(BF).reshape(2, NB, TOP)
+        return carry
+
+    def top_steps():
+        tx[...] = top_pan[...].reshape(TOP, TOP)
+        for s in range(3):
+            b, e = s * NB, (s + 1) * NB
             l_top = dot(tx[e:, b:e], uinv_ref[s]).astype(BF)
             tx[e:, b:e] = l_top
             u_pan = dot(linv_ref[s], tx[b:e, e:]).astype(BF)
             tx[b:e, e:] = u_pan
             tx[e:, e:] = (tx[e:, e:].astype(F32) - dot(l_top, u_pan)).astype(BF)
-            ux[e:, :] = (ux[e:, :].astype(F32) - dot(l_top, u_own)).astype(BF)
-
-    mycol = pl.ds(pl.multiple_of(NB * jnp.minimum(q, 3), NB), NB)
+
+    def own_steps():
+        ux[...] = top_own[...].reshape(TOP, COLS)
+        for s in range(4):
+            b, e = s * NB, (s + 1) * NB
+            u_own = dot(linv_ref[s], ux[b:e, :]).astype(BF)
+            ux[b:e, :] = u_own
+            if s < 3:
+                ux[e:, :] = (ux[e:, :].astype(F32) - dot(tx[e:, b:e], u_own)).astype(BF)
 
     TWO = 2
 
-    def below(i, carry):
+    def below_left(i, carry):
         ks = pl.ds(TWO * i, TWO)
         m = TWO * NB
+        for j in range(TWO):
+            k = TWO * i + j
+            took = moved[k][:, 0:1] > 0.5
+            left[k] = jnp.where(took, left[k].astype(F32), pan[k].astype(F32)).astype(BF)
         for s in range(4):
             b, e = s * NB, (s + 1) * NB
             l_row = dot(left[ks, :, b:e].reshape(m, NB), uinv_ref[s]).astype(BF)
@@ -581,6 +454,13 @@
             if s < 3:
                 rest = left[ks, :, e:].reshape(m, TOP - e).astype(F32)
                 left[ks, :, e:] = (rest - dot(l_row, tx[b:e, e:])).astype(BF).reshape(TWO, NB, TOP - e)
+        return carry
+
+    mycol = pl.ds(pl.multiple_of(NB * jnp.minimum(q, 3), NB), NB)
+
+    def below_rest(i, carry):
+        ks = pl.ds(TWO * i, TWO)
+        m = TWO * NB
         rest = out_ref[ks].reshape(m, COLS).astype(F32)
         rest = rest - dot(left[ks].reshape(m, TOP), ux[...])
         out_ref[ks] = rest.astype(BF).reshape(TWO, NB, COLS)
@@ -591,7 +471,112 @@
 
         return carry
 
-    lax.fori_loop(0, 8 // TWO, below, 0)
+    def ev_old_send():
+        @pl.when(r < 4)
+        def _():
+            mirror().start()
+            old_self().start()
+
+    def ev_old_got():
+        @pl.when(r < 4)
+        def _():
+            old_self().wait()
+
+        @pl.when(r >= 4)
+        def _():
+            got(old_own.at[(7 - r) % 4, pl.ds(128, 128), :], sem_mir.at[0], rem_mir.at[0], dev(7 - r, q))
+
+    def ev_piece_send():
+        @pl.when(keeps)
+        def _():
+            top_piece_self().start()
+
+        @pl.when(gives)
+        def _():
+            top_piece(0).start()
+
+        @pl.when(q < 4)
+        def _():
+            for t in range(1, 8):
+                top_piece(t).start()
+
+    def ev_piece_got():
+        @pl.when(keeps)
+        def _():
+            top_piece_self().wait()
+
+        @pl.when(jnp.logical_not(keeps))
+        def _():
+            got(top_pan.at[r, mine16, minec], sem_ts.at[0], rem_ts.at[0], dev(r, mate))
+
+        for off in range(1, NZ):
+            top_slice(off).start()
+
+    def ev_slice_got():
+        for off in range(1, NZ):
+            src = plane(off)
+            got(top_pan.at[src, mine16, minec], sem_tsl.at[0], rem_tsl.at[src], dev(r, mate))
+
+    def ev_oldsl_send():
+        @pl.when(r < 4)
+        def _():
+            old_slice_self().start()
+            for off in range(1, NZ):
+                old_slice(off).start()
+
+    def ev_oldsl_got():
+        for a in range(4):
+            @pl.when(r != a)
+            def _():
+                got(pan.at[8 + a, mine32, minec], sem_ds.at[0], rem_ds.at[a], dev(r, mate))
+
+        @pl.when(r < 4)
+        def _():
+            old_slice_self().wait()
+
+    def ev_rs0(h):
+        rs_send(h, 0, 0).start()
+        rs_send(h, 1, 0).start()
+
+    def ev_rs(h, k):
+        rs_step(h, 0, k)
+        if k < 3:
+            rs_step(h, 1, k)
+
+    todo = {
+        "C0": lambda: contribute(0), "C1": lambda: contribute(1),
+        "os": ev_old_send, "og": ev_old_got, "ps": ev_piece_send, "ph": ev_piece_got,
+        "sg": ev_slice_got, "ls": ev_oldsl_send, "lg": ev_oldsl_got,
+        "P": lambda: lax.fori_loop(0, 8, find_places, 0),
+        "X": lambda: lax.fori_loop(0, 4, displaced_own, 0),
+        "Y0": lambda: lax.fori_loop(0, 2, displaced_panel, 0),
+        "Y1": lambda: lax.fori_loop(2, 4, displaced_panel, 0),
+        "K": top_steps, "U": own_steps,
+        "L": lambda: lax.fori_loop(0, 8 // TWO, below_left, 0),
+        "F": lambda: lax.fori_loop(0, 8 // TWO, below_rest, 0),
+    }
+    for n in range(3):
+        todo["w%d" % n] = lambda n=n: raw_start(n)
+        todo["g%d" % n] = lambda n=n: raw_wait(n)
+    for h in range(2):
+        todo["r%d0" % h] = lambda h=h: ev_rs0(h)
+        for k in range(1, 4):
+            todo["r%d%d" % (h, k)] = lambda h=h, k=k: ev_rs(h, k)
+        todo["re%d" % h] = lambda h=h: rs_end(h)
+        for k in range(4):
+            todo["t%d%d" % (h, k)] = lambda h=h, k=k: zag_step(*top_z, h, k)
+            todo["d%d%d" % (h, k)] = lambda h=h, k=k: zag_step(*old_z, h, k)
+        todo["te%d" % h] = lambda h=h: zag_end(*top_z, h)
+        todo["de%d" % h] = lambda h=h: zag_end(*old_z, h)
+    for name, ring in (("R", ring_raw), ("S", ring_top), ("O", ring_old)):
+        for part in range(2):
+            for stage in range(2):
+                for verb, f in (("s", ring.start), ("f", ring.forward), ("e", ring.finish)):
+                    todo["%s%d%d%s" % (name, part, stage, verb)] = (
+                        lambda f=f, stage=stage, part=part: f(stage, part))
+            todo["%s%dc" % (name, part)] = lambda ring=ring, part=part: ring.close(part)
+    for name in ORDER:
+        todo[name]()
 
     toprow = pl.ds(pl.multiple_of(NB * jnp.minimum(r, 3), NB), NB)
 
@@ -622,8 +607,6 @@
         for off in range(1, NZ):
             old_slice(off).wait_send()
 
-    for off in range(1, NZ):
-        piece_home(off).wait_send()
     for off in range(1, NZ):
         top_slice(off).wait_send()
     for h in range(2):
@@ -634,6 +617,7 @@
                 zag(*old_z, h, way, k).wait_send()
     ring_raw.drain()
     ring_top.drain()
+    ring_old.drain()
 
 
 def local(matrix, pivots, lower_inverse, upper_inverse):
@@ -662,12 +646,10 @@
             pltpu.VMEM((8, 128, 2048), BF),
             pltpu.VMEM((8, NB, TOP), BF),
             pltpu.VMEM((8, NB, 128), F32),
-            pltpu.VMEM((8, 16, NB), BF),
-            pltpu.VMEM((8, 16, NB), BF),
             dma((14,)), dma((14,)), dma((14,)), dma((14,)), dma((14,)), dma((14,)),
             dma((24,)), dma((3,)), dma((1,)), dma((1,)), dma((6,)), dma((7,)), dma((4,)),
-            dma((8,)), dma((1,)), dma((7,)), dma((8,)), dma((7,)), dma((8,)),
-            dma((32,)), dma((32,)), dma((16,)), dma((16,)),
+            dma((8,)), dma((1,)), dma((7,)), dma((8,)),
+            dma((48,)), dma((48,)), dma((24,)), dma((24,)),
         ],
         compiler_params=pltpu.CompilerParams(
             collective_id=0, has_side_effects=True, vmem_limit_bytes=46 * 1024 * 1024),

time: 86 us -> 83.5 us (0.971)
  Pallas kernels: 81.7 us -> 79.2 us
    pallas_call x1, Pallas kernels: 81.7 us -> 79.2 us  [local(): pl.pallas_call(kernel, out_shape=jax.ShapeDtypeStruct((8, NB, COLS), BF),...]
where the time goes in v3:
time: 83.5 us; the launch traced here: 83.4 us
  Pallas kernels  79.2 us (95%)
  local copies, waits for them, and re-layouts  4.16 us (5%)
    pallas_call x1, Pallas kernels, local(): pl.pallas_call(kernel, out_shape=jax.ShapeDtypeStruct((8, NB, COLS), BF),...  79.2 us
    reshape x1, local copies, waits for them, and re-layouts, local(): rows = matrix.reshape(256, 8, 2, NB).transpose(0, 2, 1, 3)  2.12 us
    reshape x1, local copies, waits for them, and re-layouts, local(): return out.reshape(matrix.shape)  2.03 us

profile of v3, /device:TPU:1, one launch (start us, length us, event | category | flops | bytes accessed | tf_op | source)
XLA Modules:
  0.0 83.4 jit_solution(16935883146826006852)
XLA Ops:
  0.0 0.0 copy-start
  0.0 0.0 copy-start.1
  0.0 0.0 copy-start.2
  0.0 2.1 %copy.7 = bf16[256,8,2,256]{3,1,2,0:T(8,128)(2,1)S(1)} copy(bf16[256,8,2,256]{3,2,1,0:T(2,128)(2,1)} %bitcast.8) | data formatting | bytes 4194304 | tf_op jit(solution)/shard_map/reshape | solution.py:624
  2.1 0.0 copy-done
  2.1 0.0 copy-done.1
  2.2 0.0 copy-done.2
  2.2 79.2 %shard_map.46 = bf16[8,256,512]{2,1,0:T(8,128)(2,1)S(1)} custom-call(bf16[8,256,512]{2,1,0:T(8,128)(2,1)S(1)} %bitcast.7, s32[4,256]{1,0:T(4,128)S(1)} %copy-done.2, bf16[4,256,256]{2,1,0:T(8,128)(2,1)S(1)} %copy-done, bf16[4,256,256]{2,1,0:T(8,128)(2,1)S(1)} %copy-done.1), custom_call_target="tpu_custom_call" | custom-call | tf_op jit(solution)/shard_map/pallas_call | solution.py:628
  81.4 2.0 %reshape.11 = bf16[8,256,2,256]{3,2,1,0:T(2,128)(2,1)} reshape(bf16[8,256,512]{2,1,0:T(8,128)(2,1)S(1)} %shard_map.46) | data formatting | bytes 4194304 | tf_op jit(solution)/shard_map/reshape | solution.py:657
Async XLA Ops:
  0.0 2.1 %copy-start = (bf16[4,256,256]{2,1,0:T(8,128)(2,1)S(1)}, bf16[4,256,256]{2,1,0:T(8,128)(2,1)}, u32[]{:S(2)}) copy-start(bf16[4,256,256]{2,1,0:T(8,128)(2,1)} %linv_ref.1) | copy-start | bytes 1572868
  0.0 2.1 %copy-start.1 = (bf16[4,256,256]{2,1,0:T(8,128)(2,1)S(1)}, bf16[4,256,256]{2,1,0:T(8,128)(2,1)}, u32[]{:S(2)}) copy-start(bf16[4,256,256]{2,1,0:T(8,128)(2,1)} %uinv_ref.1) | copy-start | bytes 1572868
  0.0 2.2 %copy-start.2 = (s32[4,256]{1,0:T(4,128)S(1)}, s32[4,256]{1,0:T(4,128)}, u32[]{:S(2)}) copy-start(s32[4,256]{1,0:T(4,128)} %piv_ref.1) | copy-start | bytes 12292

commit v4 on v3

--- a/solution.py
+++ b/solution.py
@@ -13,7 +13,7 @@
 COLS = 512
 
 
-ORDER = ('w0', 'w1', 'w2', 'os', 'C0', 'r00', 'C1', 'r10', 'g0', 'ls', 'r01', 'g1', 'R00s', 'P', 'r11', 'lg', 'O00s', 'O10s', 'R00f', 'r02', 'r12', 'g2', 'R10s', 'R00e', 'O00f', 'O10f', 'r03', 'r13', 'R10f', 're0', 'ps', 're1', 'O00e', 'O10e', 'O01s', 'O11s', 'R10e', 'R01s', 'R11s', 'ph', 't00', 't10', 'og', 'd00', 'd10', 'O01f', 'O11f', 'sg', 'S00s', 'S10s', 't01', 't11', 'd01', 'd11', 'O01e', 'O11e', 'O0c', 'O1c', 'Y0', 'S00f', 'S10f', 'R01f', 'R11f', 't02', 't12', 'd02', 'd12', 'S00e', 'S10e', 'S01s', 'S11s', 'R01e', 'R11e', 't03', 't13', 'Y1', 'S01f', 'S11f', 'd03', 'd13', 'S01e', 'S11e', 'R0c', 'R1c', 'S0c', 'S1c', 'K', 'L', 'de0', 'de1', 'X', 'te0', 'te1', 'U', 'F')
+ORDER = ('w0', 'w1', 'w2', 'os', 'C0', 'r00', 'C1', 'r10', 'g0', 'ls', 'r01', 'g1', 'R00s', 'P', 'r11', 'lg', 'O00s', 'O10s', 'R00f', 'r02', 'r12', 'g2', 'R10s', 'R00e', 'O00f', 'O10f', 'r03', 'r13', 'og', 'd00', 'd10', 'R10f', 're0', 'ps', 're1', 'O00e', 'O10e', 'O01s', 'O11s', 'R10e', 'R01s', 'R11s', 'ph', 'd01', 'd11', 't00', 't10', 'O01f', 'O11f', 'sg', 'S00s', 'S10s', 'd02', 'd12', 't01', 't11', 'O01e', 'O11e', 'O0c', 'O1c', 'd03', 'd13', 'Y0', 'S00f', 'S10f', 'R01f', 'R11f', 't02', 't12', 'Y1', 'S00e', 'S10e', 'S01s', 'S11s', 'de0', 'de1', 'X', 'R01e', 'R11e', 't03', 't13', 'S01f', 'S11f', 'S01e', 'S11e', 'R0c', 'R1c', 'S0c', 'S1c', 'K', 'L', 'te0', 'te1', 'U', 'F')
 
 
 def dot(a, b):

time: 83.5 us -> 81.5 us (0.976)
  Pallas kernels: 79.2 us -> 77.2 us
    pallas_call x1, Pallas kernels: 79.2 us -> 77.2 us  [local(): pl.pallas_call(kernel, out_shape=jax.ShapeDtypeStruct((8, NB, COLS), BF),...]
where the time goes in v4:
time: 81.5 us; the launch traced here: 81.4 us
  Pallas kernels  77.2 us (95%)
  local copies, waits for them, and re-layouts  4.16 us (5%)
    pallas_call x1, Pallas kernels, local(): pl.pallas_call(kernel, out_shape=jax.ShapeDtypeStruct((8, NB, COLS), BF),...  77.2 us
    reshape x1, local copies, waits for them, and re-layouts, local(): rows = matrix.reshape(256, 8, 2, NB).transpose(0, 2, 1, 3)  2.12 us
    reshape x1, local copies, waits for them, and re-layouts, local(): return out.reshape(matrix.shape)  2.03 us

profile of v4, /device:TPU:1, one launch (start us, length us, event | category | flops | bytes accessed | tf_op | source)
XLA Modules:
  0.0 81.4 jit_solution(10087028371739492548)
XLA Ops:
  0.0 0.0 copy-start
  0.0 0.0 copy-start.1
  0.0 0.0 copy-start.2
  0.0 2.1 %copy.7 = bf16[256,8,2,256]{3,1,2,0:T(8,128)(2,1)S(1)} copy(bf16[256,8,2,256]{3,2,1,0:T(2,128)(2,1)} %bitcast.8) | data formatting | bytes 4194304 | tf_op jit(solution)/shard_map/reshape | solution.py:624
  2.1 0.0 copy-done
  2.1 0.0 copy-done.1
  2.2 0.0 copy-done.2
  2.2 77.2 %shard_map.46 = bf16[8,256,512]{2,1,0:T(8,128)(2,1)S(1)} custom-call(bf16[8,256,512]{2,1,0:T(8,128)(2,1)S(1)} %bitcast.7, s32[4,256]{1,0:T(4,128)S(1)} %copy-done.2, bf16[4,256,256]{2,1,0:T(8,128)(2,1)S(1)} %copy-done, bf16[4,256,256]{2,1,0:T(8,128)(2,1)S(1)} %copy-done.1), custom_call_target="tpu_custom_call" | custom-call | tf_op jit(solution)/shard_map/pallas_call | solution.py:628
  79.4 2.0 %reshape.11 = bf16[8,256,2,256]{3,2,1,0:T(2,128)(2,1)} reshape(bf16[8,256,512]{2,1,0:T(8,128)(2,1)S(1)} %shard_map.46) | data formatting | bytes 4194304 | tf_op jit(solution)/shard_map/reshape | solution.py:657
Async XLA Ops:
  0.0 2.1 %copy-start = (bf16[4,256,256]{2,1,0:T(8,128)(2,1)S(1)}, bf16[4,256,256]{2,1,0:T(8,128)(2,1)}, u32[]{:S(2)}) copy-start(bf16[4,256,256]{2,1,0:T(8,128)(2,1)} %linv_ref.1) | copy-start | bytes 1572868
  0.0 2.1 %copy-start.1 = (bf16[4,256,256]{2,1,0:T(8,128)(2,1)S(1)}, bf16[4,256,256]{2,1,0:T(8,128)(2,1)}, u32[]{:S(2)}) copy-start(bf16[4,256,256]{2,1,0:T(8,128)(2,1)} %uinv_ref.1) | copy-start | bytes 1572868
  0.0 2.2 %copy-start.2 = (s32[4,256]{1,0:T(4,128)S(1)}, s32[4,256]{1,0:T(4,128)}, u32[]{:S(2)}) copy-start(s32[4,256]{1,0:T(4,128)} %piv_ref.1) | copy-start | bytes 12292

commit v5 on v4

--- a/solution.py
+++ b/solution.py
@@ -13,7 +13,7 @@
 COLS = 512
 
 
-ORDER = ('w0', 'w1', 'w2', 'os', 'C0', 'r00', 'C1', 'r10', 'g0', 'ls', 'r01', 'g1', 'R00s', 'P', 'r11', 'lg', 'O00s', 'O10s', 'R00f', 'r02', 'r12', 'g2', 'R10s', 'R00e', 'O00f', 'O10f', 'r03', 'r13', 'og', 'd00', 'd10', 'R10f', 're0', 'ps', 're1', 'O00e', 'O10e', 'O01s', 'O11s', 'R10e', 'R01s', 'R11s', 'ph', 'd01', 'd11', 't00', 't10', 'O01f', 'O11f', 'sg', 'S00s', 'S10s', 'd02', 'd12', 't01', 't11', 'O01e', 'O11e', 'O0c', 'O1c', 'd03', 'd13', 'Y0', 'S00f', 'S10f', 'R01f', 'R11f', 't02', 't12', 'Y1', 'S00e', 'S10e', 'S01s', 'S11s', 'de0', 'de1', 'X', 'R01e', 'R11e', 't03', 't13', 'S01f', 'S11f', 'S01e', 'S11e', 'R0c', 'R1c', 'S0c', 'S1c', 'K', 'L', 'te0', 'te1', 'U', 'F')
+ORDER = ('w0', 'w1', 'w2', 'os', 'C0', 'r00', 'C1', 'r10', 'g0', 'ls', 'r01', 'g1', 'R00s', 'P', 'r11', 'lg', 'O00s', 'O10s', 'R00f', 'r02', 'r12', 'g2', 'R10s', 'R00e', 'O00f', 'O10f', 'r03', 'r13', 'og', 'd00', 'd10', 'R10f', 're0', 'ps', 're1', 'O00e', 'O10e', 'O01s', 'O11s', 'R10e', 'R01s', 'R11s', 'ph', 'd01', 'd11', 't00', 't10', 'O01f', 'O11f', 'sg', 'S00s', 'S10s', 'd02', 'd12', 't01', 't11', 'O01e', 'O11e', 'O0c', 'O1c', 'S00f', 'S10f', 'd03', 'd13', 'Y0', 'R01f', 'R11f', 't02', 't12', 'S00e', 'S10e', 'S01s', 'S11s', 'Y1', 'de0', 'de1', 't03', 't13', 'S01f', 'S11f', 'X', 'R01e', 'R11e', 'S01e', 'S11e', 'R0c', 'R1c', 'S0c', 'S1c', 'K', 'L', 'te0', 'te1', 'U', 'F')
 
 
 def dot(a, b):

time: 81.5 us -> 80.8 us (level)
  no operation moved by 1% of the time
where the time goes in v5:
time: 80.8 us; the launch traced here: 80.7 us
  Pallas kernels  76.5 us (95%)
  local copies, waits for them, and re-layouts  4.16 us (5%)
    pallas_call x1, Pallas kernels, local(): pl.pallas_call(kernel, out_shape=jax.ShapeDtypeStruct((8, NB, COLS), BF),...  76.5 us
    reshape x1, local copies, waits for them, and re-layouts, local(): rows = matrix.reshape(256, 8, 2, NB).transpose(0, 2, 1, 3)  2.12 us
    reshape x1, local copies, waits for them, and re-layouts, local(): return out.reshape(matrix.shape)  2.03 us

profile of v5, /device:TPU:1, one launch (start us, length us, event | category | flops | bytes accessed | tf_op | source)
XLA Modules:
  0.0 80.7 jit_solution(8015642777260465032)
XLA Ops:
  0.0 0.0 copy-start
  0.0 0.0 copy-start.1
  0.0 0.0 copy-start.2
  0.0 2.1 %copy.7 = bf16[256,8,2,256]{3,1,2,0:T(8,128)(2,1)S(1)} copy(bf16[256,8,2,256]{3,2,1,0:T(2,128)(2,1)} %bitcast.8) | data formatting | bytes 4194304 | tf_op jit(solution)/shard_map/reshape | solution.py:624
  2.1 0.0 copy-done
  2.1 0.0 copy-done.1
  2.2 0.0 copy-done.2
  2.2 76.5 %shard_map.46 = bf16[8,256,512]{2,1,0:T(8,128)(2,1)S(1)} custom-call(bf16[8,256,512]{2,1,0:T(8,128)(2,1)S(1)} %bitcast.7, s32[4,256]{1,0:T(4,128)S(1)} %copy-done.2, bf16[4,256,256]{2,1,0:T(8,128)(2,1)S(1)} %copy-done, bf16[4,256,256]{2,1,0:T(8,128)(2,1)S(1)} %copy-done.1), custom_call_target="tpu_custom_call" | custom-call | tf_op jit(solution)/shard_map/pallas_call | solution.py:628
  78.7 2.0 %reshape.11 = bf16[8,256,2,256]{3,2,1,0:T(2,128)(2,1)} reshape(bf16[8,256,512]{2,1,0:T(8,128)(2,1)S(1)} %shard_map.46) | data formatting | bytes 4194304 | tf_op jit(solution)/shard_map/reshape | solution.py:657
Async XLA Ops:
  0.0 2.1 %copy-start = (bf16[4,256,256]{2,1,0:T(8,128)(2,1)S(1)}, bf16[4,256,256]{2,1,0:T(8,128)(2,1)}, u32[]{:S(2)}) copy-start(bf16[4,256,256]{2,1,0:T(8,128)(2,1)} %linv_ref.1) | copy-start | bytes 1572868
  0.0 2.1 %copy-start.1 = (bf16[4,256,256]{2,1,0:T(8,128)(2,1)S(1)}, bf16[4,256,256]{2,1,0:T(8,128)(2,1)}, u32[]{:S(2)}) copy-start(bf16[4,256,256]{2,1,0:T(8,128)(2,1)} %uinv_ref.1) | copy-start | bytes 1572868
  0.0 2.2 %copy-start.2 = (s32[4,256]{1,0:T(4,128)S(1)}, s32[4,256]{1,0:T(4,128)}, u32[]{:S(2)}) copy-start(s32[4,256]{1,0:T(4,128)} %piv_ref.1) | copy-start | bytes 12292

commit v6 on v5

--- a/solution.py
+++ b/solution.py
@@ -438,7 +438,7 @@
             if s < 3:
                 ux[e:, :] = (ux[e:, :].astype(F32) - dot(tx[e:, b:e], u_own)).astype(BF)
 
-    TWO = 2
+    TWO = 4
 
     def below_left(i, carry):
         ks = pl.ds(TWO * i, TWO)

time: 80.8 us -> 79.5 us (0.984)
  Pallas kernels: 76.5 us -> 75.2 us
    pallas_call x1, Pallas kernels: 76.5 us -> 75.2 us  [local(): pl.pallas_call(kernel, out_shape=jax.ShapeDtypeStruct((8, NB, COLS), BF),...]
where the time goes in v6:
time: 79.5 us
  Pallas kernels  75.2 us (95%)
  local copies, waits for them, and re-layouts  4.16 us (5%)
    pallas_call x1, Pallas kernels, local(): pl.pallas_call(kernel, out_shape=jax.ShapeDtypeStruct((8, NB, COLS), BF),...  75.2 us
    reshape x1, local copies, waits for them, and re-layouts, local(): rows = matrix.reshape(256, 8, 2, NB).transpose(0, 2, 1, 3)  2.12 us
    reshape x1, local copies, waits for them, and re-layouts, local(): return out.reshape(matrix.shape)  2.03 us

profile of v6, /device:TPU:1, one launch (start us, length us, event | category | flops | bytes accessed | tf_op | source)
XLA Modules:
  0.0 79.5 jit_solution(6432581431109258021)
XLA Ops:
  0.0 0.0 copy-start
  0.0 0.0 copy-start.1
  0.0 0.0 copy-start.2
  0.0 2.1 %copy.7 = bf16[256,8,2,256]{3,1,2,0:T(8,128)(2,1)S(1)} copy(bf16[256,8,2,256]{3,2,1,0:T(2,128)(2,1)} %bitcast.8) | data formatting | bytes 4194304 | tf_op jit(solution)/shard_map/reshape | solution.py:624
  2.1 0.0 copy-done
  2.1 0.0 copy-done.1
  2.2 0.0 copy-done.2
  2.2 75.2 %shard_map.46 = bf16[8,256,512]{2,1,0:T(8,128)(2,1)S(1)} custom-call(bf16[8,256,512]{2,1,0:T(8,128)(2,1)S(1)} %bitcast.7, s32[4,256]{1,0:T(4,128)S(1)} %copy-done.2, bf16[4,256,256]{2,1,0:T(8,128)(2,1)S(1)} %copy-done, bf16[4,256,256]{2,1,0:T(8,128)(2,1)S(1)} %copy-done.1), custom_call_target="tpu_custom_call" | custom-call | tf_op jit(solution)/shard_map/pallas_call | solution.py:628
  77.4 2.0 %reshape.11 = bf16[8,256,2,256]{3,2,1,0:T(2,128)(2,1)} reshape(bf16[8,256,512]{2,1,0:T(8,128)(2,1)S(1)} %shard_map.46) | data formatting | bytes 4194304 | tf_op jit(solution)/shard_map/reshape | solution.py:657
Async XLA Ops:
  0.0 2.1 %copy-start = (bf16[4,256,256]{2,1,0:T(8,128)(2,1)S(1)}, bf16[4,256,256]{2,1,0:T(8,128)(2,1)}, u32[]{:S(2)}) copy-start(bf16[4,256,256]{2,1,0:T(8,128)(2,1)} %linv_ref.1) | copy-start | bytes 1572868
  0.0 2.1 %copy-start.1 = (bf16[4,256,256]{2,1,0:T(8,128)(2,1)S(1)}, bf16[4,256,256]{2,1,0:T(8,128)(2,1)}, u32[]{:S(2)}) copy-start(bf16[4,256,256]{2,1,0:T(8,128)(2,1)} %uinv_ref.1) | copy-start | bytes 1572868
  0.0 2.2 %copy-start.2 = (s32[4,256]{1,0:T(4,128)S(1)}, s32[4,256]{1,0:T(4,128)}, u32[]{:S(2)}) copy-start(s32[4,256]{1,0:T(4,128)} %piv_ref.1) | copy-start | bytes 12292
